TPU v7x, 128 devices: a whole 4x4x4 slice. The times are simulated.
128 devices in a mesh: dp: 8 (over y_lo, x), mp: 16 (over y_hi, z, core).
Axes of the slice: x: 4, y: 4 (y_hi: 2, y_lo: 2; y = y_hi * 2 + y_lo), z: 4, core: 2. Of those that a mesh axis runs over, the one named last changes fastest.
Arguments:
- tokens: bfloat16 [16384, 2304], P(('dp', 'mp')), may hold values from -6 to 6
- ada_ffn: float32 [16, 2, 2304], P('dp'), may hold values from -4 to 4
- ffn_gate: float32 [16, 2304], P('dp'), may hold values from 0.5 to 1.5
- up_weight: bfloat16 [2304, 9216], P(None, 'mp'), may hold values from -0.125 to 0.125
- up_bias: float32 [9216], P('mp'), may hold values from -6 to 6
- down_weight: bfloat16 [9216, 2304], P('mp'), may hold values from -0.125 to 0.125
- down_bias: float32 [2304], replicated, may hold values from -6 to 6
- ada_head: float32 [16, 2, 2304], P('dp'), may hold values from -4 to 4
- head_weight: bfloat16 [2304, 4096], P(None, 'mp'), may hold values from -0.125 to 0.125
- head_bias: float32 [4096], P('mp'), may hold values from -6 to 6
- gumbel_noise: float32 [8, 1024, 4096], P('dp', None, 'mp'), as said below
- codebook: bfloat16 [4096, 32], P('mp'), may hold values from -16 to 16
- phi_weight: float32 [32, 32, 3, 3], replicated, may hold values from -0.375 to 0.375
- phi_bias: float32 [32], replicated, may hold values from -6 to 6
- f_hat: float32 [8, 32, 1024], P('dp', None, 'mp'), may hold values from -6 to 6
Outputs:
- block_out: bfloat16 [16384, 2304], P(('dp', 'mp'))
- f_hat_out: float32 [8, 32, 1024], P('dp', None, 'mp')
Inputs may be any that keep to these rules, and one draw needn't show every extreme that they name: `gumbel_noise`: noise added to the guided logits.
All inputs are finite; a program needn't handle non-finite values.
Results may differ from a plain program's by a relative error of at most 0.024.
Values may be sent and summed in bfloat16 or wider, within the bound.
A program may use at most 256 MiB of HBM per device.

v0:
```python
import jax
import jax.numpy as jnp
from jax import lax
from jax.sharding import PartitionSpec as P

SIDE = 32
NEW = 1024


GUIDE = 1.5


def from_partner(value, axis, apart):
    mask = 2**apart
    pairs = [(source, source ^ mask) for source in range(lax.axis_size(axis))]
    return lax.ppermute(value, axis, pairs)


def norm_rows(values):
    row_mean = jnp.mean(values, axis=-1, keepdims=True)
    centred = values - row_mean
    spread = jnp.mean(centred * centred, axis=-1, keepdims=True)
    return centred * lax.rsqrt(spread + 1e-06)


def per_image(lookup, row_images):
    picked = jnp.broadcast_to(lookup[0], (row_images.shape[0],) + lookup.shape[1:])
    chosen = (row_images == 1).reshape((-1,) + (1,) * (lookup.ndim - 1))
    picked = jnp.where(chosen, lookup[1], picked)
    return picked


def modulate(values, ada_rows):
    return (norm_rows(values) * (1.0 + ada_rows[:, 1]) + ada_rows[:, 0]).astype(jnp.bfloat16)


def body(
    tokens,
    ada_ffn,
    ffn_gate,
    up_weight,
    up_bias,
    down_weight,
    down_bias,
    ada_head,
    head_weight,
    head_bias,
    gumbel_noise,
    codebook,
    phi_weight,
    phi_bias,
    f_hat,
):
    row_count = tokens.shape[0]
    shard_count = lax.axis_size("mp")
    mp_index = lax.axis_index("mp")
    group_rows = row_count * shard_count
    own_images = (mp_index * row_count + jnp.arange(row_count, dtype=jnp.int32)) // NEW
    gathered = lax.all_gather(tokens, "mp", axis=0, tiled=True)
    row_images = jnp.arange(group_rows, dtype=jnp.int32) // NEW
    full_hidden = jax.nn.gelu(
        jnp.dot(
            modulate(gathered.astype(jnp.float32), per_image(ada_ffn, row_images)),
            up_weight,
            preferred_element_type=jnp.float32,
        )
        + up_bias,
        approximate=True,
    ).astype(jnp.bfloat16)
    summed = lax.psum_scatter(
        jnp.dot(full_hidden, down_weight, preferred_element_type=jnp.float32),
        "mp",
        scatter_dimension=0,
        tiled=True,
    )
    block_out = (
        tokens.astype(jnp.float32) + per_image(ffn_gate, own_images) * (summed + down_bias)
    ).astype(jnp.bfloat16)
    full_out = lax.all_gather(block_out, "mp", axis=0, tiled=True)
    logits = (
        jnp.dot(
            modulate(full_out.astype(jnp.float32), per_image(ada_head, row_images)),
            head_weight,
            preferred_element_type=jnp.float32,
        )
        + head_bias
    )
    half_rows = group_rows // 2
    upper_half = lax.axis_index("dp") // (lax.axis_size("dp") // 2)
    kept_rows = lax.dynamic_slice_in_dim(logits, upper_half * half_rows, half_rows, 0)
    sent_rows = lax.dynamic_slice_in_dim(logits, (1 - upper_half) * half_rows, half_rows, 0)
    twin_rows = from_partner(sent_rows, "dp", lax.axis_size("dp").bit_length() - 2)
    cond_rows = jnp.where(upper_half == 0, kept_rows, twin_rows)
    uncond_rows = jnp.where(upper_half == 0, twin_rows, kept_rows)
    scores = (1.0 + GUIDE) * cond_rows - GUIDE * uncond_rows + gumbel_noise.reshape(half_rows, -1)
    row_peak = jnp.max(scores, axis=1)
    weights = jnp.exp(scores - row_peak[:, None]).astype(jnp.bfloat16)
    row_total = jnp.sum(weights.astype(jnp.float32), axis=1)
    mixed_code = jnp.dot(weights, codebook, preferred_element_type=jnp.float32)
    global_peak = lax.pmax(row_peak, "mp")
    factor = jnp.exp(row_peak - global_peak)
    row_total, mixed_code = (
        lax.psum((row_total * factor).astype(jnp.bfloat16), "mp").astype(jnp.float32),
        lax.psum((mixed_code * factor[:, None]).astype(jnp.bfloat16), "mp").astype(jnp.float32),
    )
    soft_code = mixed_code / row_total[:, None]
    pair_count = f_hat.shape[0]
    channels = f_hat.shape[1]
    band_rows = f_hat.shape[2] // SIDE
    code_maps = soft_code.reshape(pair_count, SIDE, SIDE, channels)
    padded = jnp.pad(code_maps, ((0, 0), (1, 1), (1, 1), (0, 0)))
    window = lax.dynamic_slice_in_dim(padded, mp_index * band_rows, band_rows + 2, 1)
    conv_out = (
        jnp.zeros((pair_count, channels, band_rows, SIDE), jnp.float32)
        + phi_bias[None, :, None, None]
    )
    for row_step in range(3):
        for col_step in range(3):
            conv_out = conv_out + jnp.einsum(
                "pyxc,oc->poyx",
                window[:, row_step : row_step + band_rows, col_step : col_step + SIDE, :],
                phi_weight[:, :, row_step, col_step],
                precision=lax.Precision.HIGHEST,
            )
    own_cells = jnp.transpose(window[:, 1 : band_rows + 1, 1 : SIDE + 1, :], (0, 3, 1, 2))
    f_hat_out = f_hat + (0.5 * own_cells + 0.5 * conv_out).reshape(
        pair_count, channels, band_rows * SIDE
    )
    return (block_out, f_hat_out)


def solution(mesh):
    in_specs = (
        P(("dp", "mp"), None),
        P("dp", None, None),
        P("dp", None),
        P(None, "mp"),
        P("mp"),
        P("mp", None),
        P(),
        P("dp", None, None),
        P(None, "mp"),
        P("mp"),
        P("dp", None, "mp"),
        P("mp", None),
        P(),
        P(),
        P("dp", None, "mp"),
    )
    out_specs = (P(("dp", "mp"), None), P("dp", None, "mp"))
    return jax.shard_map(body, mesh=mesh, in_specs=in_specs, out_specs=out_specs, check_vma=False)
```

profile of v0, /device:TPU:1, one launch (start us, length us, event | category | flops | bytes accessed | tf_op | source)
XLA Modules:
  0.0 590.0 jit_solution(9555418837395056854)
XLA Ops:
  7.2 0.0 copy-start
  7.2 0.0 all-gather.3.cloned.1.call-start
  7.2 0.7 all-gather.3.cloned.1.call-update
  7.9 0.0 reduce-scatter.2.cloned.1.call-start
  8.0 0.8 slice_bitcast_fusion.3
  8.8 24.7 %broadcast_select_fusion = (f32[2048,2,2304]{2,0,1:T(8,128)}, f32[2048,2,2304]{2,0,1:T(8,128)}) fusion(f32[2,2304]{1,0:T(2,128)S(1)} %get-tuple-element.9, f32[2,2304]{1,0:T(2,128)S(1)} %get-tuple-element.8, pred[2048]{0:T(1024)(128)(4,1)S(1)} %fusion.70, f32[2,2304]{1,0:T(2,128)S(1)} %get-tuple-element.14, f32[2,2304]{1,0:T(2,128)S(1)} %get-tuple-element.15), kind=kLoop, calls=%fused_computation.22 | loop fusion | flops 18874368 | bytes 75573248 | tf_op jit(solution)/shard_map/jit(_where)/select_n | solution.py:29
  33.4 0.0 copy-start.13
  33.4 58.3 %all-gather.3.cloned.1.call-done = bf16[2048,2304]{1,0:T(8,128)(2,1)} async-done(((bf16[128,2304]{1,0:T(8,128)(2,1)}), bf16[2048,2304]{1,0:T(8,128)(2,1)}) %all-gather.3.cloned.1.call-update) | async-done | bytes 9437200 | tf_op jit(solution)/shard_map/all_gather | solution.py:59
  91.8 0.0 copy-start.3
  91.8 5.1 convert_reduce_fusion.1
  96.9 1.2 copy-done.3
  98.1 2.6 fusion.8
  100.7 0.0 copy-done
  100.7 0.0 copy-done.13
  100.7 28.5 %fusion.29 = f32[2048,2304]{1,0:T(8,128)} fusion(bf16[576,2304]{1,0:T(8,128)(2,1)S(1)} %copy-done, bf16[2304,576]{0,1:T(8,128)(2,1)} %param.18, bf16[2048,2304]{1,0:T(8,128)(2,1)} %all-gather.3.cloned.1.call-done, f32[2048,2,2304]{2,0,1:T(8,128)} %get-tuple-element.13, f32[2048]{0:T(1024)S(1)} %add_rsqrt_fusion.1, f32[2048]{0:T(1024)S(1)} %broadcast_multiply_fusion.1, ...), kind=kOutput, calls=%fused_computation.35 | convolution fusion | flops 10916462592 | bytes 71387392 | tf_op jit(solution)/shard_map/dot_general | solution.py:71
  129.3 0.0 reduce-scatter.2.cloned.1.call-update
  129.3 0.0 all-gather.5.cloned.1.call-start
  129.4 0.6 copy-done.7
  130.0 155.1 %reduce-scatter.2.cloned.1.call-done = f32[128,2304]{1,0:T(8,128)} async-done(((f32[2048,2304]{1,0:T(8,128)}), f32[128,2304]{1,0:T(8,128)}) %reduce-scatter.2.cloned.1.call-update) | async-done | bytes 1179664 | tf_op jit(solution)/shard_map/reduce_scatter | solution.py:70
  285.1 0.0 copy-done.4
  285.1 0.0 copy-done.10
  285.1 2.4 add_convert_fusion
  287.5 0.0 all-gather.5.cloned.1.call-update
  287.5 0.2 all-reduce.3.cloned.1.call-start
  287.8 0.0 copy-start.14
  287.8 76.8 %all-gather.5.cloned.1.call-done = bf16[2048,2304]{1,0:T(8,128)(2,1)} async-done(((bf16[128,2304]{1,0:T(8,128)(2,1)}), bf16[2048,2304]{1,0:T(8,128)(2,1)}) %all-gather.5.cloned.1.call-update) | async-done | bytes 9437200 | tf_op jit(solution)/shard_map/all_gather | solution.py:79
  364.6 5.1 convert_reduce_fusion
  369.8 1.2 copy-done.2
  371.0 2.6 fusion.4
  373.6 0.0 copy-done.14
  373.6 0.0 copy-done.12
  373.6 0.0 copy-start.1
  373.6 14.0 %fusion.31 = f32[2048,256]{0,1:T(8,128)S(1)} fusion(bf16[2304,256]{1,0:T(8,128)(2,1)S(1)} %copy-done.12, bf16[2048,2304]{1,0:T(8,128)(2,1)S(1)} %copy-done.2, f32[2048,2,2304]{2,0,1:T(8,128)} %get-tuple-element.12, f32[2048]{0:T(1024)S(1)} %add_rsqrt_fusion, f32[2048]{0:T(1024)S(1)} %broadcast_multiply_fusion, f32[256]{0:T(256)S(1)} %copy-done.14), kind=kOutput, calls=%fused_computation.36 | convolution fusion | flops 2449473536 | bytes 50480128 | tf_op jit(solution)/shard_map/dot_general | solution.py:81
  387.6 0.0 copy-start.5
  387.7 1.3 copy-done.5
  389.0 1.1 constant_dynamic-slice_fusion
  390.1 0.3 collective-permute-start
  390.4 2.5 copy.17
  392.9 22.0 %collective-permute-done = f32[1024,256]{0,1:T(8,128)} collective-permute-done((f32[1024,256]{0,1:T(8,128)}, f32[1024,256]{0,1:T(8,128)}, u32[]{:S(2)}, u32[]{:S(2)}) %collective-permute-start) | collective-permute-done | bytes 1048608 | tf_op jit(solution)/shard_map/ppermute | solution.py:16
  414.9 3.3 fusion.97
  418.1 33.6 %pmax.7 = f32[1024]{0:T(1024)S(1)} all-reduce(f32[1024]{0:T(1024)S(1)} %get-tuple-element.6), channel_id=1, replica_groups=mesh['dp'=8,'mp'=16] {'mp'}, use_global_device_ids=true, to_apply=%region_6.7 | all-reduce | flops 1024 | bytes 8192 | tf_op jit(solution)/shard_map/pmax | solution.py:100
  451.7 1.4 convert_reduce_fusion.2
  453.1 0.0 copy-done.8
  453.1 2.1 fusion.39
  455.2 0.0 all-reduce.3.cloned.1.call-update
  455.3 33.6 %psum.15 = bf16[1024]{0:T(1024)(128)(2,1)S(1)} all-reduce(bf16[1024]{0:T(1024)(128)(2,1)S(1)} %get-tuple-element.4), channel_id=1, replica_groups=mesh['dp'=8,'mp'=16] {'mp'}, use_global_device_ids=true, to_apply=%region_9.10 | all-reduce | flops 1024 | bytes 4096 | tf_op jit(solution)/shard_map/psum | solution.py:103
  488.9 91.2 %all-reduce.3.cloned.1.call-done = bf16[1024,32]{0,1:T(8,128)(2,1)} async-done(((bf16[1024,32]{0,1:T(8,128)(2,1)}), bf16[1024,32]{0,1:T(8,128)(2,1)}) %all-reduce.3.cloned.1.call-update) | async-done | bytes 65552 | tf_op jit(solution)/shard_map/psum | solution.py:104
  580.1 0.9 convert_divide_fusion
  580.9 0.2 copy.20
  581.1 0.0 copy-done.6
  581.1 0.0 copy-done.11
  581.1 0.2 convolution_add_fusion.8
  581.3 0.2 convolution_add_fusion.7
  581.5 0.2 convolution_add_fusion.6
  581.7 0.2 convolution_add_fusion.5
  581.8 0.2 convolution_add_fusion.4
  582.0 0.2 convolution_add_fusion.3
  582.2 0.2 convolution_add_fusion.2
  582.4 0.2 convolution_add_fusion.1
  582.6 0.2 fusion.42
  582.8 0.1 copy.19
  582.8 0.0 copy-done.9
  582.8 0.6 add.204
  583.4 0.0 copy-done.1
  (18 shorter events, 0.1 us)
Async XLA Ops:
  7.2 93.6 %copy-start = (bf16[576,2304]{1,0:T(8,128)(2,1)S(1)}, bf16[576,2304]{1,0:T(8,128)(2,1)}, u32[]{:S(2)}) copy-start(bf16[576,2304]{1,0:T(8,128)(2,1)} %param.20) | copy-start | bytes 7962628
  7.2 84.6 %all-gather.3.cloned.1.call-start = ((), (), s32[]{:S(2)}) async-start(), calls=%async_computation.1 | async-start | bytes 10027008 | tf_op jit(solution)/shard_map/all_gather | solution.py:59
  7.9 277.2 %reduce-scatter.2.cloned.1.call-start = ((), (), s32[]{:S(2)}) async-start(), calls=%async_computation.2 | async-start | bytes 20054016 | tf_op jit(solution)/shard_map/reduce_scatter | solution.py:70
  33.4 67.3 %copy-start.13 = (f32[576]{0:T(1024)S(1)}, f32[576]{0:T(1024)}, u32[]{:S(2)}) copy-start(f32[576]{0:T(1024)} %param.19) | copy-start | bytes 6916
  91.8 6.4 %copy-start.3 = (bf16[2048,2304]{1,0:T(8,128)(2,1)S(1)}, bf16[2048,2304]{1,0:T(8,128)(2,1)}, u32[]{:S(2)}) copy-start(bf16[2048,2304]{1,0:T(8,128)(2,1)} %all-gather.3.cloned.1.call-done) | copy-start | bytes 28311556
  129.3 0.7 copy-start.7
  129.3 155.9 %copy-start.4 = (bf16[128,2304]{1,0:T(8,128)(2,1)S(1)}, bf16[128,2304]{1,0:T(8,128)(2,1)}, u32[]{:S(2)}) copy-start(bf16[128,2304]{1,0:T(8,128)(2,1)} %param.15) | copy-start | bytes 1769476
  129.3 155.9 %copy-start.10 = (f32[2304]{0:T(1024)S(1)}, f32[2304]{0:T(1024)}, u32[]{:S(2)}) copy-start(f32[2304]{0:T(1024)} %param.21) | copy-start | bytes 27652
  129.3 235.3 %all-gather.5.cloned.1.call-start = ((), (), s32[]{:S(2)}) async-start(), calls=%async_computation.3 | async-start | bytes 10027008 | tf_op jit(solution)/shard_map/all_gather | solution.py:79
  287.5 292.5 %all-reduce.3.cloned.1.call-start = ((), (), s32[]{:S(2)}) async-start(), calls=%async_computation.4 | async-start | bytes 131072 | tf_op jit(solution)/shard_map/psum | solution.py:104
  287.8 85.8 %copy-start.14 = (f32[256]{0:T(256)S(1)}, f32[256]{0:T(256)}, u32[]{:S(2)}) copy-start(f32[256]{0:T(256)} %param.24) | copy-start | bytes 3076
  364.6 6.4 %copy-start.2 = (bf16[2048,2304]{1,0:T(8,128)(2,1)S(1)}, bf16[2048,2304]{1,0:T(8,128)(2,1)}, u32[]{:S(2)}) copy-start(bf16[2048,2304]{1,0:T(8,128)(2,1)} %all-gather.5.cloned.1.call-done) | copy-start | bytes 28311556
  364.6 9.0 %copy-start.12 = (bf16[2304,256]{1,0:T(8,128)(2,1)S(1)}, bf16[2304,256]{1,0:T(8,128)(2,1)}, u32[]{:S(2)}) copy-start(bf16[2304,256]{1,0:T(8,128)(2,1)} %param.23) | copy-start | bytes 3538948
  373.6 209.8 %copy-start.1 = (bf16[576,2304]{1,0:T(8,128)(2,1)S(1)}, bf16[576,2304]{1,0:T(8,128)(2,1)}, u32[]{:S(2)}) copy-start(bf16[576,2304]{1,0:T(8,128)(2,1)} %param.20) | copy-start | bytes 7962628
  387.6 1.4 copy-start.5
  389.0 64.1 %copy-start.8 = (bf16[256,32]{0,1:T(8,128)(2,1)S(1)}, bf16[256,32]{0,1:T(8,128)(2,1)}, u32[]{:S(2)}) copy-start(bf16[256,32]{0,1:T(8,128)(2,1)} %param.26) | copy-start | bytes 49156
  389.0 192.1 %copy-start.6 = (f32[32,32,3,3]{1,0,3,2:T(8,128)S(1)}, f32[32,32,3,3]{1,0,3,2:T(8,128)}, u32[]{:S(2)}) copy-start(f32[32,32,3,3]{1,0,3,2:T(8,128)} %param.27) | copy-start | bytes 110596
  389.0 192.1 %copy-start.11 = (f32[32]{0:T(128)S(1)}, f32[32]{0:T(128)}, u32[]{:S(2)}) copy-start(f32[32]{0:T(128)} %param.28) | copy-start | bytes 388
  389.0 193.8 %copy-start.9 = (f32[1,32,64]{2,1,0:T(8,128)S(1)}, f32[1,32,64]{2,1,0:T(8,128)}, u32[]{:S(2)}) copy-start(f32[1,32,64]{2,1,0:T(8,128)} %param.29) | copy-start | bytes 24580
  390.1 24.8 %collective-permute-start = (f32[1024,256]{0,1:T(8,128)}, f32[1024,256]{0,1:T(8,128)}, u32[]{:S(2)}, u32[]{:S(2)}) collective-permute-start(f32[1024,256]{0,1:T(8,128)} %constant_dynamic-slice_fusion), channel_id=1, source_target_pairs={{0,64},{16,80},{32,96},{48,112},{64,0},{80,16},{96,32},{112,48},{1... | collective-permute-start | bytes 3145736 | tf_op jit(solution)/shard_map/ppermute | solution.py:16
Sparse Core Ops, SparseCore 0:
  10.5 81.2 all-gather.2
  129.4 155.6 reduce-scatter.1
  288.2 76.3 all-gather.4
  455.4 124.6 all-reduce.2
where the time goes:
time: 591 us; the launch traced here: 590 us
  waiting for transfers between devices  404 us (68%)
  blocking collectives  67.2 us (11%)
  other arithmetic  48.6 us (8%)
  matrix products  46.2 us (8%)
  between operations  14 us (2%)
  local copies, waits for them, and re-layouts  9.16 us (2%)
    reduce_scatter x1, waiting for transfers between devices, body(): lax.psum_scatter(jnp.dot(full_hidden, down_weight, preferred_element_type...  155 us
    psum x1, waiting for transfers between devices, body(): lax.psum((mixed_code * factor[:, None]).astype(jnp.bfloat16), 'mp')  91.2 us
    all_gather x1, waiting for transfers between devices, body(): full_out = lax.all_gather(block_out, 'mp', axis=0, tiled=True)  76.8 us
    all_gather x1, waiting for transfers between devices, body(): gathered = lax.all_gather(tokens, 'mp', axis=0, tiled=True)  58.3 us
    psum x1, blocking collectives, body(): lax.psum((row_total * factor).astype(jnp.bfloat16), 'mp')  33.6 us
    pmax x1, blocking collectives, body(): global_peak = lax.pmax(row_peak, 'mp')  33.6 us
    dot_general x1, matrix products, body(): jnp.dot(full_hidden, down_weight, preferred_element_type=jnp.float32)  28.5 us
    select_n x1, other arithmetic, per_image(): picked = jnp.where(chosen, lookup[1], picked)  24.7 us
  transfers between devices with their start and end apart: 5, of which 5 were waited for; matrix products, arithmetic and copies ran while one was open for 5% of the time, Pallas kernels for 0%

commit v1 on v0

v1 whole, which is shorter than its diff:
```python
import functools

import jax
import jax.numpy as jnp
from jax import lax
from jax.experimental import pallas as pl
from jax.experimental.pallas import tpu as pltpu
from jax.sharding import PartitionSpec as P

MESH = pl.DeviceIdType.MESH
BF = jnp.bfloat16
F32 = jnp.float32

D = 2304
ROWS = 128
HID = 576
UNITS = 3
UK = D // UNITS
UQ = UK // 4
CW = D // UNITS
DQ = HID // 4
SIDE = 32
VB = 256
MSG = 40
GUIDE = 1.5


def position():
    dp, mp = lax.axis_index("dp"), lax.axis_index("mp")
    return dp // 4, dp % 4, mp // 8, (mp // 2) % 4, mp % 2


def device(ylo, x, yhi, z, core):
    return (ylo * 4 + x, yhi * 8 + z * 2 + core)


def remote(src, dst, send, recv, target):
    return pltpu.make_async_remote_copy(
        src_ref=src, dst_ref=dst, send_sem=send, recv_sem=recv, device_id=target, device_id_type=MESH
    )


def norm_rows(values):
    centred = values - jnp.mean(values, axis=-1, keepdims=True)
    spread = jnp.mean(centred * centred, axis=-1, keepdims=True)
    return centred * lax.rsqrt(spread + 1e-06)


def gelu(v):
    return 0.5 * v * (1.0 + jnp.tanh(0.7978845608028654 * (v + 0.044715 * v * v * v)))


def greet(targets):
    barrier = pltpu.get_barrier_semaphore()
    for target in targets:
        pl.semaphore_signal(barrier, inc=1, device_id=target, device_id_type=MESH)
    return lambda: pl.semaphore_wait(barrier, len(targets))


def ffn_kernel(
    tok, ada, gate, up_w, up_b, down_w, down_b, out,
    xn, up, dn, ub, hid, part, opp, nxt, got1, got2,
    loc_s, y_s, y_r, a_s, a_r, b_s, b_r, c_s, c_r, o_s, o_r, z_s, z_r, bias_s, bias_r, p_s, p_r, q_s, q_r,
):
    ylo, x, yhi, z, core = position()
    sib = device(ylo, x, yhi, z, 1 - core)
    partner = device(1 - ylo, x, 1 - yhi, z, core)
    partner_sib = device(1 - ylo, x, 1 - yhi, z, 1 - core)
    xr, xl = device(ylo, (x + 1) % 4, yhi, z, core), device(ylo, (x + 3) % 4, yhi, z, core)
    zr_i, zl_i, zo_i = (z + 1) % 4, (z + 3) % 4, (z + 2) % 4
    zr, zl = device(ylo, x, yhi, zr_i, core), device(ylo, x, yhi, zl_i, core)
    arrived = greet([sib, partner, partner_sib, xr, xl, zr, zl])

    local = [pltpu.make_async_copy(up_w, up.at[0], loc_s.at[0])]
    for j in range(UNITS):
        local.append(pltpu.make_async_copy(down_w.at[:, pl.ds(j * CW, CW)], dn.at[j, 0], loc_s.at[1 + j]))
    local[0].start()

    @pl.loop(0, ROWS // 16)
    def _(i):
        rows = pl.ds(pl.multiple_of(i * 16, 16), 16)
        pair = ada[yhi]
        v = norm_rows(tok[rows, :].astype(F32)) * (1.0 + pair[1:2, :]) + pair[0:1, :]
        xn[z, rows, :] = v.astype(BF)

    arrived()

    def y_copy(k):
        if k < UNITS:
            rows = pl.ds(pl.multiple_of(k * UK + x * UQ, 16), UQ)
            return remote(up_w.at[rows, :], up.at[2, rows, :], y_s.at[k], y_r.at[k], partner)
        j = k - UNITS
        rows = pl.ds(pl.multiple_of(x * DQ, 16), DQ)
        return remote(
            down_w.at[rows, pl.ds(j * CW, CW)], dn.at[j, 2, rows, :], y_s.at[k], y_r.at[k], partner
        )

    def piece(k, q, half=None):
        if k < UNITS:
            if half is None:
                return up.at[2, pl.ds(pl.multiple_of(k * UK + q * UQ, 16), UQ), :]
            return up.at[2, pl.ds(pl.multiple_of(k * UK + q * UQ + half * (UQ // 2), 16), UQ // 2), :]
        rows = pl.ds(pl.multiple_of(q * DQ, 16), DQ)
        if half is None:
            return dn.at[k - UNITS, 2, rows, :]
        return dn.at[k - UNITS, 2, rows, pl.ds(half * (CW // 2), CW // 2)]

    x_l, x_r = (x + 3) % 4, (x + 1) % 4

    def a_copies(k):
        ref = piece(k, x)
        return [
            remote(ref, ref, a_s.at[k, 0], a_r.at[k, 0], xr),
            remote(ref, ref, a_s.at[k, 1], a_r.at[k, 1], xl),
        ]

    def b_copies(k):
        from_left, from_right = piece(k, x_l, 0), piece(k, x_r, 1)
        return [
            remote(from_left, from_left, b_s.at[k, 0], b_r.at[k, 0], xr),
            remote(from_right, from_right, b_s.at[k, 1], b_r.at[k, 1], xl),
        ]

    def c_copy(k):
        if k < UNITS:
            rows = pl.ds(k * UK, UK)
            return remote(up.at[2, rows, :], up.at[3, rows, :], c_s.at[k], c_r.at[k], sib)
        return remote(dn.at[k - UNITS, 2], dn.at[k - UNITS, 3], c_s.at[k], c_r.at[k], sib)

    y = [y_copy(k) for k in range(2 * UNITS)]
    a = [a_copies(k) for k in range(2 * UNITS)]
    b = [b_copies(k) for k in range(2 * UNITS)]
    c = [c_copy(k) for k in range(2 * UNITS)]
    y[0].start()
    z1 = [
        remote(xn.at[z], xn.at[z], z_s.at[0], z_r.at[0], zr),
        remote(xn.at[z], xn.at[z], z_s.at[1], z_r.at[1], zl),
    ]
    z2 = [
        remote(xn.at[zl_i, pl.ds(0, 64)], xn.at[zl_i, pl.ds(0, 64)], z_s.at[2], z_r.at[2], zr),
        remote(xn.at[zr_i, pl.ds(64, 64)], xn.at[zr_i, pl.ds(64, 64)], z_s.at[3], z_r.at[3], zl),
    ]
    for cp in z1:
        cp.start()
    y[1].start()
    own_up = remote(up_w, up.at[1], o_s.at[0], o_r.at[0], sib)
    own_up.start()
    own_dn = [
        remote(down_w.at[:, pl.ds(j * CW, CW)], dn.at[j, 1], o_s.at[1 + j], o_r.at[1 + j], sib)
        for j in range(UNITS)
    ]
    pltpu.make_async_copy(up_b, ub.at[0], loc_s.at[4]).start()
    biases = [
        remote(up_b, ub.at[1], bias_s.at[0], bias_r.at[0], sib),
        remote(up_b, ub.at[2], bias_s.at[1], bias_r.at[1], partner),
        remote(up_b, ub.at[3], bias_s.at[2], bias_r.at[2], partner_sib),
    ]
    for cp in biases:
        cp.start()

    def hidden(first):
        @pl.loop(0, 4)
        def _(i):
            p, m = first + i // 2, i % 2
            lhs = xn[pl.ds(2 * m, 2)].reshape(256, D)
            acc = jnp.dot(lhs, up[p], preferred_element_type=F32)
            hid[p, pl.ds(pl.multiple_of(m * 256, 256), 256), :] = gelu(acc + ub[p]).astype(BF)

    def partial(j):
        @pl.loop(0, 2)
        def _(m):
            rows = pl.ds(pl.multiple_of(m * 256, 256), 256)
            acc = jnp.dot(hid[0, rows, :], dn[j, 0], preferred_element_type=F32)
            for p in range(1, 4):
                acc = acc + jnp.dot(hid[p, rows, :], dn[j, p], preferred_element_type=F32)
            part[j, pl.ds(2 * m, 2)] = acc.reshape(2, ROWS, CW)

        opp[j] = part[j, zo_i].astype(BF)
        for cp in p1(j):
            cp.start()

    def p1(j):
        return [
            remote(opp.at[j, pl.ds(0, 64)], got1.at[j, 0], p_s.at[j, 0], p_r.at[j, 0], zr),
            remote(opp.at[j, pl.ds(64, 64)], got1.at[j, 1], p_s.at[j, 1], p_r.at[j, 1], zl),
        ]

    def p2(j):
        return [
            remote(nxt.at[j, 0], got2.at[j, 0], q_s.at[j, 0], q_r.at[j, 0], zr),
            remote(nxt.at[j, 1], got2.at[j, 1], q_s.at[j, 1], q_r.at[j, 1], zl),
        ]

    def second(j):
        for cp in p1(j):
            cp.wait_recv()
        nxt[j, 0, 0:64] = (part[j, zr_i, 0:64] + got1[j, 0].astype(F32)).astype(BF)
        nxt[j, 0, 64:128] = part[j, zr_i, 64:128].astype(BF)
        nxt[j, 1, 0:64] = part[j, zl_i, 0:64].astype(BF)
        nxt[j, 1, 64:128] = (part[j, zl_i, 64:128] + got1[j, 1].astype(F32)).astype(BF)
        for cp in p2(j):
            cp.start()

    def finish(j):
        for cp in p2(j):
            cp.wait_recv()
        cols = pl.ds(j * CW, CW)
        total = part[j, z] + got2[j, 0].astype(F32) + got2[j, 1].astype(F32)
        total = total + down_b[:, cols]
        out[:, cols] = (tok[:, cols].astype(F32) + gate[pl.ds(yhi, 1), cols] * total).astype(BF)

    last = 2 * UNITS - 1

    def tick(k):
        if k <= last:
            y[k].wait_recv()
            for cp in a[k]:
                cp.start()
            if k + 2 <= last:
                y[k + 2].start()
        if 0 <= k - 1 <= last:
            for cp in a[k - 1]:
                cp.wait_recv()
            for cp in b[k - 1]:
                cp.start()
        if 0 <= k - 2 <= last:
            for cp in b[k - 2]:
                cp.wait_recv()
            c[k - 2].start()

    tick(0)
    tick(1)
    for cp in local[1:]:
        cp.start()
    for cp in own_dn:
        cp.start()
    for cp in z1:
        cp.wait_recv()
    for cp in z2:
        cp.start()
    tick(2)
    for cp in z2:
        cp.wait_recv()
    local[0].wait()
    own_up.wait_recv()
    pltpu.make_async_copy(up_b, ub.at[0], loc_s.at[4]).wait()
    for cp in biases:
        cp.wait_recv()
    hidden(0)
    tick(3)
    tick(4)
    for k in range(UNITS):
        c[k].wait_recv()
    hidden(2)
    tick(5)
    for cp in local[1:]:
        cp.wait()
    for cp in own_dn:
        cp.wait_recv()
    c[3].wait_recv()
    partial(0)
    tick(6)
    c[4].wait_recv()
    partial(1)
    second(0)
    tick(7)
    c[5].wait_recv()
    partial(2)
    second(1)
    second(2)
    for j in range(UNITS):
        finish(j)

    for cp in y + c + z1 + z2 + [own_up] + own_dn + biases:
        cp.wait_send()
    for group in a + b + [p1(j) for j in range(UNITS)] + [p2(j) for j in range(UNITS)]:
        for cp in group:
            cp.wait_send()


def ffn_block(tokens, ada, gate, up_w, up_b, down_w, down_b):
    dma = pltpu.SemaphoreType.DMA
    units = 2 * UNITS
    vmem, anywhere = pl.BlockSpec(memory_space=pltpu.VMEM), pl.BlockSpec(memory_space=pl.ANY)
    return pl.pallas_call(
        ffn_kernel,
        out_shape=jax.ShapeDtypeStruct((ROWS, D), BF),
        in_specs=[vmem, vmem, vmem, anywhere, vmem, anywhere, vmem],
        out_specs=vmem,
        scratch_shapes=[
            pltpu.VMEM((4, ROWS, D), BF),
            pltpu.VMEM((4, D, HID), BF),
            pltpu.VMEM((UNITS, 4, HID, CW), BF),
            pltpu.VMEM((4, 1, HID), F32),
            pltpu.VMEM((4, 512, HID), BF),
            pltpu.VMEM((UNITS, 4, ROWS, CW), F32),
            pltpu.VMEM((UNITS, ROWS, CW), BF),
            pltpu.VMEM((UNITS, 2, ROWS, CW), BF),
            pltpu.VMEM((UNITS, 2, ROWS // 2, CW), BF),
            pltpu.VMEM((UNITS, 2, ROWS, CW), BF),
            dma((5,)),
            dma((units,)), dma((units,)),
            dma((units, 2)), dma((units, 2)),
            dma((units, 2)), dma((units, 2)),
            dma((units,)), dma((units,)),
            dma((1 + UNITS,)), dma((1 + UNITS,)),
            dma((4,)), dma((4,)),
            dma((3,)), dma((3,)),
            dma((UNITS, 2)), dma((UNITS, 2)),
            dma((UNITS, 2)), dma((UNITS, 2)),
        ],
        name="ffn_block",
        compiler_params=pltpu.CompilerParams(
            collective_id=1, has_side_effects=True, vmem_limit_bytes=60 * 1024 * 1024
        ),
    )(tokens, ada, gate, up_w, up_b.reshape(1, -1), down_w, down_b.reshape(1, -1))


def head_kernel(
    blk, ada, head_w, head_b, noise, book, phi, phi_b, f_hat, out,
    h, mine, theirs, g, book_x, stage, turned, got,
    t_s, t_r, y_s, y_r, l_s, z_s, z_r, w_s, w_r, c_s, c_r, m_s, m_r,
):
    ylo, x, yhi, z, core = position()
    dp, mp = lax.axis_index("dp"), lax.axis_index("mp")
    sib = device(ylo, x, yhi, z, 1 - core)
    twin = device(1 - ylo, x, yhi, z, core)
    partner = device(1 - ylo, x, 1 - yhi, z, core)
    zr_i, zl_i, zo_i = (z + 1) % 4, (z + 3) % 4, (z + 2) % 4
    zr, zl = device(ylo, x, yhi, zr_i, core), device(ylo, x, yhi, zl_i, core)
    arrived = greet([twin, partner] + [(dp, (mp + o) % 16) for o in range(1, 16)])

    @pl.loop(0, ROWS // 16)
    def _(i):
        rows = pl.ds(pl.multiple_of(i * 16, 16), 16)
        pair = ada[yhi]
        v = norm_rows(blk[rows, :].astype(F32)) * (1.0 + pair[1:2, :]) + pair[0:1, :]
        h[rows, :] = v.astype(BF)

    book_x[...] = jnp.where(lax.broadcasted_iota(jnp.int32, (VB, 128), 1) == SIDE, 1.0, 0.0).astype(BF)
    book_x[:, 0:32] = book[...]
    arrived()

    lo = pl.multiple_of(ylo * 64, 64)
    other = pl.multiple_of((1 - ylo) * 64, 64)
    t = [
        remote(
            h.at[pl.ds(pl.multiple_of(other + k * CR, CR), CR)], theirs.at[pl.ds(k * CR, CR)],
            t_s.at[k], t_r.at[k], twin,
        )
        for k in range(NCH)
    ]
    for cp in t:
        cp.start()
    same = ylo == yhi
    home = device(yhi, x, yhi, z, core)
    away = device(yhi, x, 1 - yhi, z, core)
    own_weight = jnp.where(ylo == 0, 1.0 + GUIDE, -GUIDE)
    twin_weight = jnp.where(ylo == 0, -GUIDE, 1.0 + GUIDE)

    def slot(k, zi, half):
        return g.at[zi, core, half, pl.ds(k * CR, CR)]

    def away_copy(k):
        return remote(mine.at[pl.ds(k * CR, CR)], slot(k, z, ylo), y_s.at[k, 0], y_r.at[k, ylo], away)

    def home_copy(k):
        return remote(mine.at[pl.ds(k * CR, CR)], slot(k, z, ylo), y_s.at[k, 1], y_r.at[k, ylo], home)

    def stay_copy(k):
        return pltpu.make_async_copy(mine.at[pl.ds(k * CR, CR)], slot(k, z, ylo), l_s.at[k])

    def z1(k):
        return [
            remote(slot(k, z, i), slot(k, z, i), z_s.at[k, d, i], z_r.at[k, d, i], target)
            for d, target in ((0, zr), (1, zl)) for i in range(2)
        ]

    def z2(k):
        return [
            remote(slot(k, zl_i, 0), slot(k, zl_i, 0), w_s.at[k, 0], w_r.at[k, 0], zr),
            remote(slot(k, zr_i, 1), slot(k, zr_i, 1), w_s.at[k, 1], w_r.at[k, 1], zl),
        ]

    def cross(k, step, zi):
        return [
            remote(slot(k, zi, i), slot(k, zi, i), c_s.at[k, step, i], c_r.at[k, step, i], sib)
            for i in range(2)
        ]

    def mix(k):
        t[k].wait_recv()
        rows = pl.ds(k * CR, CR)
        own = h[pl.ds(pl.multiple_of(lo + k * CR, CR), CR), :].astype(F32)
        mine[rows, :] = (own_weight * own + twin_weight * theirs[rows, :].astype(F32)).astype(BF)
        away_copy(k).start()

        @pl.when(same)
        def _():
            stay_copy(k).start()

        @pl.when(jnp.logical_not(same))
        def _():
            home_copy(k).start()

    def gathered(k):
        @pl.when(same)
        def _():
            stay_copy(k).wait()
            remote(mine.at[pl.ds(k * CR, CR)], slot(k, z, 1 - ylo), y_s.at[k, 0], y_r.at[k, 1 - ylo], away).wait_recv()

        @pl.when(jnp.logical_not(same))
        def _():
            for i in range(2):
                remote(mine.at[pl.ds(k * CR, CR)], slot(k, z, i), y_s.at[k, 0], y_r.at[k, i], away).wait_recv()

        for cp in z1(k) + cross(k, 0, z):
            cp.start()

    def second(k):
        for cp in z1(k):
            cp.wait_recv()
        for cp in z2(k) + cross(k, 1, zr_i) + cross(k, 2, zl_i):
            cp.start()

    def third(k):
        for cp in z2(k):
            cp.wait_recv()
        for cp in cross(k, 3, zo_i):
            cp.start()

    for k in range(NCH + 3):
        if k < NCH:
            mix(k)
        if 0 <= k - 1 < NCH:
            gathered(k - 1)
        if 0 <= k - 2 < NCH:
            second(k - 2)
        if 0 <= k - 3 < NCH:
            third(k - 3)
    for k in range(NCH):
        for cp in cross(k, 0, z) + cross(k, 1, zr_i) + cross(k, 2, zl_i) + cross(k, 3, zo_i):
            cp.wait_recv()

    @pl.loop(0, 4)
    def _(i):
        rows = pl.ds(pl.multiple_of(i * 256, 256), 256)
        lhs = g[pl.ds(i, 1)].reshape(256, D)
        scores = jnp.dot(lhs, head_w[...], preferred_element_type=F32) + head_b[...] + noise[0, rows, :]
        peak = jnp.max(scores, axis=1, keepdims=True)
        weights = jnp.exp(scores - peak).astype(BF)
        code = jnp.dot(weights, book_x[...], preferred_element_type=F32)
        code = jnp.where(lax.broadcasted_iota(jnp.int32, code.shape, 1) == SIDE + 1, peak, code)
        flipped = jnp.transpose(code)
        turned[:, pl.ds(pl.multiple_of(128 + i * 256, 128), 256)] = flipped[0:MSG, :]

    zeros = jnp.zeros((MSG, 128), F32)
    turned[:, 0:128] = zeros
    turned[:, 1152:1280] = zeros
    cells = turned[...]
    for parity, shift in ((0, 96), (1, 32)):
        rolled = pltpu.roll(cells, 1280 - shift, 1)
        for i in range(8):
            to = 2 * i + parity
            start = (128 + 64 * to - 32 - shift)
            stage[to] = rolled[:, start:start + 128]

    posts = []
    for o in range(1, 16):
        to = (mp + o) % 16
        cp = remote(stage.at[to], got.at[o], m_s.at[o], m_r.at[o], (dp, to))
        cp.start()
        posts.append(cp)
    got[0] = stage[mp]
    for cp in posts:
        cp.wait_recv()
    peaks = got[:, SIDE + 1:SIDE + 2, :]
    factor = jnp.exp(peaks - jnp.max(peaks, axis=0, keepdims=True))
    sums = jnp.sum(got[:, 0:MSG, :] * factor, axis=0)
    lane = lax.broadcasted_iota(jnp.int32, (1, 128), 1)
    outside = jnp.logical_or(jnp.logical_and(mp == 0, lane < 32), jnp.logical_and(mp == 15, lane >= 96))
    soft = jnp.where(outside, 0.0, sums[0:32] / jnp.where(outside, 1.0, sums[32:33]))
    taps = []
    for i in range(3):
        for j in range(3):
            offset = 32 * (i - 1) + (j - 1)
            tap = soft if offset == 0 else pltpu.roll(soft, (-offset) % 128, 1)
            if j == 0:
                tap = jnp.where(lane % 32 == 0, 0.0, tap)
            if j == 2:
                tap = jnp.where(lane % 32 == 31, 0.0, tap)
            taps.append(tap)
    conv = jnp.dot(
        phi[...], jnp.concatenate(taps, axis=0), preferred_element_type=F32, precision=lax.Precision.HIGHEST
    )
    total = 0.5 * soft + 0.5 * (conv + phi_b[...])
    out[0] = f_hat[0] + pltpu.roll(total, 96, 1)[:, 0:64]

    for cp in t + posts:
        cp.wait_send()
    for k in range(NCH):
        away_copy(k).wait_send()

        @pl.when(jnp.logical_not(same))
        def _():
            home_copy(k).wait_send()

        for cp in z1(k) + z2(k) + cross(k, 0, z) + cross(k, 1, zr_i) + cross(k, 2, zl_i) + cross(k, 3, zo_i):
            cp.wait_send()


NCH = 2
CR = 64 // NCH


def head_block(block_out, ada, head_w, head_b, noise, book, phi, phi_b, f_hat):
    dma = pltpu.SemaphoreType.DMA
    vmem = pl.BlockSpec(memory_space=pltpu.VMEM)
    return pl.pallas_call(
        head_kernel,
        out_shape=jax.ShapeDtypeStruct((1, 32, 64), F32),
        in_specs=[vmem] * 9,
        out_specs=vmem,
        scratch_shapes=[
            pltpu.VMEM((ROWS, D), BF),
            pltpu.VMEM((64, D), BF),
            pltpu.VMEM((64, D), BF),
            pltpu.VMEM((4, 2, 2, 64, D), BF),
            pltpu.VMEM((VB, 128), BF),
            pltpu.VMEM((16, MSG, 128), F32),
            pltpu.VMEM((MSG, 1280), F32),
            pltpu.VMEM((16, MSG, 128), F32),
            dma((NCH,)), dma((NCH,)),
            dma((NCH, 2)), dma((NCH, 2)),
            dma((NCH,)),
            dma((NCH, 2, 2)), dma((NCH, 2, 2)),
            dma((NCH, 2)), dma((NCH, 2)),
            dma((NCH, 4, 2)), dma((NCH, 4, 2)),
            dma((16,)), dma((16,)),
        ],
        name="head_block",
        compiler_params=pltpu.CompilerParams(
            collective_id=2, has_side_effects=True, vmem_limit_bytes=60 * 1024 * 1024
        ),
    )(
        block_out, ada, head_w, head_b.reshape(1, -1), noise, book,
        jnp.transpose(phi, (0, 2, 3, 1)).reshape(32, 288), phi_b.reshape(32, 1), f_hat,
    )


def body(
    tokens, ada_ffn, ffn_gate, up_weight, up_bias, down_weight, down_bias, ada_head,
    head_weight, head_bias, gumbel_noise, codebook, phi_weight, phi_bias, f_hat,
):
    block_out = ffn_block(tokens, ada_ffn, ffn_gate, up_weight, up_bias, down_weight, down_bias)
    f_hat_out = head_block(
        block_out, ada_head, head_weight, head_bias, gumbel_noise, codebook, phi_weight, phi_bias, f_hat
    )
    return (block_out, f_hat_out)


def solution(mesh):
    in_specs = (
        P(("dp", "mp"), None),
        P("dp", None, None),
        P("dp", None),
        P(None, "mp"),
        P("mp"),
        P("mp", None),
        P(),
        P("dp", None, None),
        P(None, "mp"),
        P("mp"),
        P("dp", None, "mp"),
        P("mp", None),
        P(),
        P(),
        P("dp", None, "mp"),
    )
    out_specs = (P(("dp", "mp"), None), P("dp", None, "mp"))
    return jax.shard_map(body, mesh=mesh, in_specs=in_specs, out_specs=out_specs, check_vma=False)
```

time: 591 us -> 152 us (0.26)
  waiting for transfers between devices: 404 us -> 0 us
  Pallas kernels: 0 us -> 141 us
  blocking collectives: 67.2 us -> 0 us
  other arithmetic: 48.6 us -> 0 us
  matrix products: 46.2 us -> 0 us
  between operations: 14 us -> 0.7 us
    reduce_scatter x1 -> x0, waiting for transfers between devices: 155 us -> none  [body(): lax.psum_scatter(jnp.dot(full_hidden, down_weight, preferred_element_type...]
    pallas_call x0 -> x2, Pallas kernels: none -> 141 us  [the longest x1 88.3 us: ffn_block(): pl.pallas_call(ffn_kernel, out_shape=jax.ShapeDtypeStruct((ROWS, D), BF),...]
    all_gather x2 -> x0, waiting for transfers between devices: 135 us -> none  [the longest x1 76.8 us: body(): full_out = lax.all_gather(block_out, 'mp', axis=0, tiled=True)]
    psum x1 -> x0, waiting for transfers between devices: 91.2 us -> none  [body(): lax.psum((mixed_code * factor[:, None]).astype(jnp.bfloat16), 'mp')]
    dot_general x12 -> x0, matrix products: 46.2 us -> none  [the longest x1 28.5 us: body(): jnp.dot(full_hidden, down_weight, preferred_element_type=jnp.float32)]
    psum x1 -> x0, blocking collectives: 33.6 us -> none  [body(): lax.psum((row_total * factor).astype(jnp.bfloat16), 'mp')]
    pmax x1 -> x0, blocking collectives: 33.6 us -> none  [body(): global_peak = lax.pmax(row_peak, 'mp')]
    select_n x1 -> x0, other arithmetic: 24.7 us -> none  [per_image(): picked = jnp.where(chosen, lookup[1], picked)]
  transfers between devices with their start and end apart: 5 -> 0, of which waited for: 5 -> 0; matrix products, arithmetic and copies ran while one was open for 5% -> 0% of each run, Pallas kernels for 0% -> 0%
where the time goes in v1:
time: 152 us
  Pallas kernels  141 us (93%)
  local copies, waits for them, and re-layouts  10.2 us (7%)
    pallas_call x1, Pallas kernels, ffn_block(): pl.pallas_call(ffn_kernel, out_shape=jax.ShapeDtypeStruct((ROWS, D), BF),...  88.3 us
    pallas_call x1, Pallas kernels, head_block(): pl.pallas_call(head_kernel, out_shape=jax.ShapeDtypeStruct((1, 32, 64), F...  53 us
    unnamed x16, local copies, waits for them, and re-layouts  7.41 us

profile of v1, /device:TPU:1, one launch (start us, length us, event | category | flops | bytes accessed | tf_op | source)
XLA Modules:
  0.0 152.1 jit_solution(16563818575995782355)
XLA Ops:
  0.6 0.0 copy-start.3
  0.6 0.0 copy-start.4
  0.7 4.5 %copy.21.up_w = bf16[2304,576]{1,0:T(8,128)(2,1)} copy(bf16[2304,576]{0,1:T(8,128)(2,1)} %param.18) | data formatting | bytes 5308416 | tf_op args[3]
  5.2 0.0 copy-done.3
  5.2 0.6 reshape.20.down_b
  5.8 0.0 copy-done.4
  5.8 0.6 reshape.19.up_b
  6.4 0.0 copy-start.1
  6.4 0.0 copy-start.2
  6.4 0.0 copy-start.5
  6.4 88.3 %ffn_block.1.blk = bf16[128,2304]{1,0:T(8,128)(2,1)} custom-call(bf16[128,2304]{1,0:T(8,128)(2,1)} %tok.1, f32[2,2,2304]{2,1,0:T(2,128)} %ada.2, f32[2,2304]{1,0:T(2,128)} %gate.1, bf16[2304,576]{1,0:T(8,128)(2,1)} %copy.21.up_w, f32[1,576]{1,0:T(1,128)} %reshape.19.up_b, bf16[576,2304]{1,0:T(8,128)(2,1)} %down_w.1, f32[1,2304]{1,0:T(1,128)} %reshape.20.down_b), custom_call_target="tpu_custom_call" | custom-call | tf_op jit(solution)/shard_map/ffn_block/pallas_call | solution.py:285
  94.6 0.0 copy-start
  94.6 0.0 copy-done.1
  94.7 0.1 copy.22
  94.8 0.8 reshape.22.phi
  95.5 0.0 copy-done.2
  95.5 0.7 copy.23.book
  96.3 0.0 copy-done.5
  96.3 0.7 copy.24.phi_b
  97.0 53.0 %head_block.1 = f32[1,32,64]{2,1,0:T(8,128)} custom-call(bf16[128,2304]{1,0:T(8,128)(2,1)} %ffn_block.1.blk, f32[2,2,2304]{2,1,0:T(2,128)} %ada.3, bf16[2304,256]{1,0:T(8,128)(2,1)} %head_w.1, f32[1,256]{1,0:T(1,128)} %bitcast.4, f32[1,1024,256]{2,1,0:T(8,128)} %noise.1, bf16[256,32]{1,0:T(8,128)(2,1)} %copy.23.book, f32[32,288]{1,0:T(8,128)} %reshape.22.phi, ...), custom_call_target="tpu_custom_call" | custom-call | tf_op jit(solution)/shard_map/head_block/pallas_call | solution.py:519
  149.9 0.0 copy-done
  149.9 0.8 copy.27
  150.8 1.3 copy.28
Async XLA Ops:
  0.6 4.5 %copy-start.3 = (f32[2304]{0:T(1024)S(1)}, f32[2304]{0:T(1024)}, u32[]{:S(2)}) copy-start(f32[2304]{0:T(1024)} %param.21) | copy-start | bytes 27652
  0.6 5.1 %copy-start.4 = (f32[576]{0:T(1024)S(1)}, f32[576]{0:T(1024)}, u32[]{:S(2)}) copy-start(f32[576]{0:T(1024)} %param.19) | copy-start | bytes 6916
  6.4 88.3 %copy-start.1 = (f32[32,32,3,3]{1,0,3,2:T(8,128)S(1)}, f32[32,32,3,3]{1,0,3,2:T(8,128)}, u32[]{:S(2)}) copy-start(f32[32,32,3,3]{1,0,3,2:T(8,128)} %param.27) | copy-start | bytes 110596
  6.4 89.2 %copy-start.2 = (bf16[256,32]{0,1:T(8,128)(2,1)S(1)}, bf16[256,32]{0,1:T(8,128)(2,1)}, u32[]{:S(2)}) copy-start(bf16[256,32]{0,1:T(8,128)(2,1)} %param.26) | copy-start | bytes 49156
  6.4 89.9 %copy-start.5 = (f32[32]{0:T(128)S(1)}, f32[32]{0:T(128)}, u32[]{:S(2)}) copy-start(f32[32]{0:T(128)} %param.28) | copy-start | bytes 388
  94.6 55.3 %copy-start = (bf16[128,2304]{1,0:T(8,128)(2,1)S(1)}, bf16[128,2304]{1,0:T(8,128)(2,1)}, u32[]{:S(2)}) copy-start(bf16[128,2304]{1,0:T(8,128)(2,1)} %ffn_block.1.blk) | copy-start | bytes 1769476

commit v2 on v1

v2 whole, which is shorter than its diff:
```python
import functools

import jax
import jax.numpy as jnp
from jax import lax
from jax.experimental import pallas as pl
from jax.experimental.pallas import tpu as pltpu
from jax.sharding import PartitionSpec as P

MESH = pl.DeviceIdType.MESH
BF = jnp.bfloat16
F32 = jnp.float32

D = 2304
ROWS = 128
HID = 576
FOREIGN = 2 * HID
DQ = HID // 4
UNITS = (
    ("ring", "up", 0, 128),
    ("ring", "up", 128, 192),
    ("ring", "up", 320, 256),
    ("twin", "down", 0, 512),
    ("ring", "down", 512, 768),
    ("ring", "down", 1280, 512),
    ("twin", "down", 1792, 512),
)
PUSHED = (0, 1, 2, 3, 4, 5, 6)
NU = len(UNITS)
CHUNKS = tuple(k for k in range(NU) if UNITS[k][1] == "down")
NC = len(CHUNKS)
STEPS = (
    ("y", 0), ("a", 0), ("y", 1), ("b", 0), ("z", 1),
    ("y", 2), ("a", 1), ("z", 2), ("tile", 0), ("y", 3),
    ("tile", 1), ("tile", 2), ("a", 2), ("tile", 3), ("early", 0),
    ("early", 1), ("b", 1), ("early", 2), ("y", 4), ("early", 3),
    ("b", 2), ("a", 3), ("y", 5), ("late", 0), ("tile", 4),
    ("tile", 5), ("tile", 6), ("tile", 7), ("tile", 8), ("a", 4),
    ("first", 0), ("y", 6), ("a", 5), ("second", 0), ("b", 4),
    ("first", 1), ("b", 5), ("finish", 0), ("first", 2), ("a", 6),
    ("second", 1), ("first", 3), ("second", 2), ("finish", 1), ("second", 3),
    ("finish", 2), ("finish", 3),
)
NARROW = 256
FIRST = 1024
SIDE = 32
VB = 256
MSG = 40
GUIDE = 1.5


def position():
    dp, mp = lax.axis_index("dp"), lax.axis_index("mp")
    return dp // 4, dp % 4, mp // 8, (mp // 2) % 4, mp % 2


def device(ylo, x, yhi, z, core):
    return (ylo * 4 + x, yhi * 8 + z * 2 + core)


def remote(src, dst, send, recv, target):
    return pltpu.make_async_remote_copy(
        src_ref=src, dst_ref=dst, send_sem=send, recv_sem=recv, device_id=target, device_id_type=MESH
    )


def norm_rows(values):
    centred = values - jnp.mean(values, axis=-1, keepdims=True)
    spread = jnp.mean(centred * centred, axis=-1, keepdims=True)
    return centred * lax.rsqrt(spread + 1e-06)


def gelu(v):
    return 0.5 * v * (1.0 + jnp.tanh(0.7978845608028654 * (v + 0.044715 * v * v * v)))


def greet(targets):
    barrier = pltpu.get_barrier_semaphore()
    for target in targets:
        pl.semaphore_signal(barrier, inc=1, device_id=target, device_id_type=MESH)
    return lambda: pl.semaphore_wait(barrier, len(targets))


def ffn_part(
    arrived, tok, ada, gate, up_w, up_b, down_w, down_b, out,
    xn, up, dns, ub, bias_row, hid, parts, opps, nbrs, gots,
    loc_s, y_s, y_r, a_s, a_r, b_s, b_r, c_s, c_r, o_s, o_r, z_s, z_r, bias_s, bias_r,
    p_s, p_r, q_s, q_r,
):
    ylo, x, yhi, z, core = position()
    sib = device(ylo, x, yhi, z, 1 - core)
    partner = device(1 - ylo, x, 1 - yhi, z, core)
    partner_sib = device(1 - ylo, x, 1 - yhi, z, 1 - core)
    twin = device(1 - ylo, x, yhi, z, core)
    x_l, x_r = (x + 3) % 4, (x + 1) % 4
    xr, xl = device(ylo, x_r, yhi, z, core), device(ylo, x_l, yhi, z, core)
    zr_i, zl_i, zo_i = (z + 1) % 4, (z + 3) % 4, (z + 2) % 4
    zr, zl = device(ylo, x, yhi, zr_i, core), device(ylo, x, yhi, zl_i, core)

    own_rows, sib_rows = pl.ds(0, HID), pl.ds(HID, HID)

    def cols(j):
        return pl.ds(UNITS[CHUNKS[j]][2], UNITS[CHUNKS[j]][3])

    loc_up = pltpu.make_async_copy(up_w, up.at[own_rows], loc_s.at[0])
    loc_up.start()
    loc_dn = [
        pltpu.make_async_copy(down_w.at[:, cols(j)], dns[j].at[own_rows], loc_s.at[3 + j]) for j in range(NC)
    ]
    loc_bias = pltpu.make_async_copy(up_b, ub.at[0], loc_s.at[2])
    loc_bias.start()

    @pl.loop(0, ROWS // 16)
    def _(i):
        rows = pl.ds(pl.multiple_of(i * 16, 16), 16)
        pair = ada[yhi]
        v = norm_rows(tok[rows, :].astype(F32)) * (1.0 + pair[1:2, :]) + pair[0:1, :]
        xn[z, rows, :] = v.astype(BF)

    arrived()

    def part_of(k, count, index, foreign=True):
        way, panel, first, size = UNITS[k]
        base = FOREIGN if foreign else 0
        if panel == "up":
            rows = pl.ds(pl.multiple_of(base + first + index * (size // count), 16), size // count)
            return (up if foreign else up_w).at[rows]
        rows = pl.ds(pl.multiple_of(base + index * (HID // count), 16), HID // count)
        return dns[CHUNKS.index(k)].at[rows] if foreign else down_w.at[rows, pl.ds(first, size)]

    def half_of(k, index, half):
        way, panel, first, size = UNITS[k]
        if panel == "up":
            rows = pl.ds(pl.multiple_of(FOREIGN + first + index * (size // 4), 16), size // 4)
            return up.at[rows, pl.ds(half * (D // 2), D // 2)]
        rows = pl.ds(pl.multiple_of(FOREIGN + index * DQ, 16), DQ)
        return dns[CHUNKS.index(k)].at[rows, pl.ds(half * (size // 2), size // 2)]

    def whole(k, base):
        way, panel, first, size = UNITS[k]
        if panel == "up":
            return up.at[pl.ds(base + first, size)]
        return dns[CHUNKS.index(k)].at[pl.ds(base, HID)]

    y, a, b, c = [], [], [], []
    for k in range(NU):
        c.append(remote(whole(k, FOREIGN), whole(k, FOREIGN + HID), c_s.at[k], c_r.at[k], sib))
        if UNITS[k][0] == "ring":
            own = part_of(k, 4, x)
            y.append(remote(part_of(k, 4, x, False), own, y_s.at[k], y_r.at[k], partner))
            a.append([
                remote(own, own, a_s.at[k, 0], a_r.at[k, 0], xr), remote(own, own, a_s.at[k, 1], a_r.at[k, 1], xl)
            ])
            from_l, from_r = half_of(k, x_l, 0), half_of(k, x_r, 1)
            b.append([
                remote(from_l, from_l, b_s.at[k, 0], b_r.at[k, 0], xr),
                remote(from_r, from_r, b_s.at[k, 1], b_r.at[k, 1], xl),
            ])
        else:
            y.append(remote(
                part_of(k, 2, 1 - ylo, False), part_of(k, 2, 1 - ylo), y_s.at[k], y_r.at[k], partner
            ))
            own = part_of(k, 2, ylo)
            a.append([remote(own, own, a_s.at[k, 0], a_r.at[k, 0], twin)])
            b.append([])

    z1 = [
        remote(xn.at[z], xn.at[z], z_s.at[0], z_r.at[0], zr),
        remote(xn.at[z], xn.at[z], z_s.at[1], z_r.at[1], zl),
    ]
    z2 = [
        remote(xn.at[zl_i, pl.ds(0, 64)], xn.at[zl_i, pl.ds(0, 64)], z_s.at[2], z_r.at[2], zr),
        remote(xn.at[zr_i, pl.ds(64, 64)], xn.at[zr_i, pl.ds(64, 64)], z_s.at[3], z_r.at[3], zl),
    ]
    own_up = remote(up_w, up.at[sib_rows], o_s.at[0], o_r.at[0], sib)
    own_dn = [
        remote(down_w.at[:, cols(j)], dns[j].at[sib_rows], o_s.at[1 + j], o_r.at[1 + j], sib) for j in range(NC)
    ]
    biases = [
        remote(up_b, ub.at[1], bias_s.at[0], bias_r.at[0], sib),
        remote(up_b, ub.at[2], bias_s.at[1], bias_r.at[1], partner),
        remote(up_b, ub.at[3], bias_s.at[2], bias_r.at[2], partner_sib),
    ]

    def start(*copies):
        for cp in copies:
            cp.start()

    def recv(*copies):
        for cp in copies:
            cp.wait_recv()

    def hidden(n):
        units = pl.ds(n * NARROW, NARROW)

        @pl.loop(0, 2)
        def _(m):
            rows = pl.ds(pl.multiple_of(m * 256, 256), 256)
            acc = lax.dot_general(
                xn[pl.ds(2 * m, 2)].reshape(256, D), up[units, :], (((1,), (1,)), ((), ())),
                preferred_element_type=F32,
            )
            hid[rows, units] = gelu(acc + bias_row[:, units]).astype(BF)

    def partial(j, late):
        units = pl.ds(FIRST, D - FIRST) if late else pl.ds(0, FIRST)
        width = UNITS[CHUNKS[j]][3]

        @pl.loop(0, 2)
        def _(m):
            rows = pl.ds(pl.multiple_of(m * 256, 256), 256)
            acc = jnp.dot(hid[rows, units], dns[j][units], preferred_element_type=F32).reshape(2, ROWS, width)
            if late:
                acc = acc + parts[j][pl.ds(2 * m, 2)]
            parts[j][pl.ds(2 * m, 2)] = acc

    low, high = pl.ds(0, 64), pl.ds(64, 64)

    p1 = [
        [
            remote(opps[j].at[low], gots[j].at[0, 0], p_s.at[j, 0, 0], p_r.at[j, 0, 0], zr),
            remote(opps[j].at[high], gots[j].at[1, 0], p_s.at[j, 1, 0], p_r.at[j, 1, 0], zl),
        ]
        for j in range(NC)
    ]
    ind = [
        [
            remote(nbrs[j].at[0, 0], gots[j].at[0, 1], p_s.at[j, 0, 1], p_r.at[j, 0, 1], zr),
            remote(nbrs[j].at[1, 0], gots[j].at[1, 1], p_s.at[j, 1, 1], p_r.at[j, 1, 1], zl),
        ]
        for j in range(NC)
    ]
    p2 = [
        [
            remote(nbrs[j].at[0, 1], gots[j].at[0, 2], q_s.at[j, 0], q_r.at[j, 0], zr),
            remote(nbrs[j].at[1, 1], gots[j].at[1, 2], q_s.at[j, 1], q_r.at[j, 1], zl),
        ]
        for j in range(NC)
    ]

    def reduce_first(j):
        recv(c[CHUNKS[j]])
        partial(j, True)
        opps[j][...] = parts[j][zo_i].astype(BF)
        start(*p1[j])
        nbrs[j][0, 0] = parts[j][zr_i, high].astype(BF)
        nbrs[j][1, 0] = parts[j][zl_i, low].astype(BF)
        start(*ind[j])

    def reduce_second(j):
        recv(*p1[j])
        nbrs[j][0, 1] = (parts[j][zr_i, low] + gots[j][0, 0].astype(F32)).astype(BF)
        nbrs[j][1, 1] = (parts[j][zl_i, high] + gots[j][1, 0].astype(F32)).astype(BF)
        start(*p2[j])

    def finish(j):
        recv(*ind[j], *p2[j])
        for rows, left, right in ((low, 2, 1), (high, 1, 2)):
            total = parts[j][z, rows] + gots[j][0, left].astype(F32) + gots[j][1, right].astype(F32)
            total = total + down_b[:, cols(j)]
            out[rows, cols(j)] = (
                tok[rows, cols(j)].astype(F32) + gate[pl.ds(yhi, 1), cols(j)] * total
            ).astype(BF)

    start(y[PUSHED[0]], *z1, *biases, own_up)
    for cp in loc_dn:
        cp.start()
    y[PUSHED[0]].wait_send()
    start(y[PUSHED[1]], y[PUSHED[2]])
    for op, k in STEPS:
        if op == "y":
            recv(y[k])
            start(*a[k])
            at = PUSHED.index(k)
            if 0 < at < NU - 2:
                start(y[PUSHED[at + 2]])
        elif op == "a":
            recv(*a[k])
            start(*(b[k] if UNITS[k][0] == "ring" else [c[k]]))
        elif op == "b":
            recv(*b[k])
            start(c[k])
        elif op == "z" and k == 1:
            recv(*z1)
            start(*z2, *own_dn)
        elif op == "z":
            loc_bias.wait()
            recv(*biases)
            bias_row[...] = jnp.concatenate([ub[i] for i in range(4)], axis=1)
            loc_up.wait()
            recv(own_up, *z2)
        elif op == "early":
            loc_dn[k].wait()
            recv(own_dn[k])
            partial(k, False)
        elif op == "tile":
            hidden(k)
        elif op == "late":
            recv(*[c[i] for i in range(NU) if UNITS[i][1] == "up"])
        elif op == "first":
            reduce_first(k)
        elif op == "second":
            reduce_second(k)
        else:
            finish(k)

    y[PUSHED[0]] = None
    for cp in [v for v in y if v is not None] + c + z1 + z2 + [own_up] + own_dn + biases:
        cp.wait_send()
    for group in a + b + p1 + ind + p2:
        for cp in group:
            cp.wait_send()


def head_part(
    blk, ada, head_w, head_b, noise, phi, phi_b, f_hat, out,
    h, mine, theirs, g, book_x, stage, turned, got,
    t_s, t_r, y_s, y_r, l_s, z_s, z_r, w_s, w_r, c_s, c_r, m_s, m_r,
):
    ylo, x, yhi, z, core = position()
    dp, mp = lax.axis_index("dp"), lax.axis_index("mp")
    sib = device(ylo, x, yhi, z, 1 - core)
    twin = device(1 - ylo, x, yhi, z, core)
    partner = device(1 - ylo, x, 1 - yhi, z, core)
    zr_i, zl_i, zo_i = (z + 1) % 4, (z + 3) % 4, (z + 2) % 4
    zr, zl = device(ylo, x, yhi, zr_i, core), device(ylo, x, yhi, zl_i, core)
    lo = pl.multiple_of(ylo * 64, 64)
    other = pl.multiple_of((1 - ylo) * 64, 64)
    t = [
        remote(
            h.at[pl.ds(pl.multiple_of(other + k * CR, CR), CR)], theirs.at[pl.ds(k * CR, CR)],
            t_s.at[k], t_r.at[k], twin,
        )
        for k in range(NCH)
    ]
    pair = ada[yhi]

    def normalise(rows):
        v = norm_rows(blk[rows, :].astype(F32)) * (1.0 + pair[1:2, :]) + pair[0:1, :]
        h[rows, :] = v.astype(BF)

    for k in range(NCH):
        normalise(pl.ds(pl.multiple_of(other + k * CR, CR), CR))
        t[k].start()
    for k in range(NCH):
        normalise(pl.ds(pl.multiple_of(lo + k * CR, CR), CR))
    same = ylo == yhi
    home = device(yhi, x, yhi, z, core)
    away = device(yhi, x, 1 - yhi, z, core)
    own_weight = jnp.where(ylo == 0, 1.0 + GUIDE, -GUIDE)
    twin_weight = jnp.where(ylo == 0, -GUIDE, 1.0 + GUIDE)

    def slot(k, zi, half):
        return g.at[zi, core, half, pl.ds(k * CR, CR)]

    def away_copy(k):
        return remote(mine.at[pl.ds(k * CR, CR)], slot(k, z, ylo), y_s.at[k, 0], y_r.at[k, ylo], away)

    def home_copy(k):
        return remote(mine.at[pl.ds(k * CR, CR)], slot(k, z, ylo), y_s.at[k, 1], y_r.at[k, ylo], home)

    def stay_copy(k):
        return pltpu.make_async_copy(mine.at[pl.ds(k * CR, CR)], slot(k, z, ylo), l_s.at[k])

    def z1(k):
        return [
            remote(slot(k, z, i), slot(k, z, i), z_s.at[k, d, i], z_r.at[k, d, i], target)
            for d, target in ((0, zr), (1, zl)) for i in range(2)
        ]

    def z2(k):
        return [
            remote(slot(k, zl_i, 0), slot(k, zl_i, 0), w_s.at[k, 0], w_r.at[k, 0], zr),
            remote(slot(k, zr_i, 1), slot(k, zr_i, 1), w_s.at[k, 1], w_r.at[k, 1], zl),
        ]

    def cross(k, step, zi):
        return [
            remote(slot(k, zi, i), slot(k, zi, i), c_s.at[k, step, i], c_r.at[k, step, i], sib)
            for i in range(2)
        ]

    def mix(k):
        t[k].wait_recv()
        rows = pl.ds(k * CR, CR)
        own = h[pl.ds(pl.multiple_of(lo + k * CR, CR), CR), :].astype(F32)
        mine[rows, :] = (own_weight * own + twin_weight * theirs[rows, :].astype(F32)).astype(BF)
        away_copy(k).start()

        @pl.when(same)
        def _():
            stay_copy(k).start()

        @pl.when(jnp.logical_not(same))
        def _():
            home_copy(k).start()

    def gathered(k):
        @pl.when(same)
        def _():
            stay_copy(k).wait()
            remote(mine.at[pl.ds(k * CR, CR)], slot(k, z, 1 - ylo), y_s.at[k, 0], y_r.at[k, 1 - ylo], away).wait_recv()

        @pl.when(jnp.logical_not(same))
        def _():
            for i in range(2):
                remote(mine.at[pl.ds(k * CR, CR)], slot(k, z, i), y_s.at[k, 0], y_r.at[k, i], away).wait_recv()

        for cp in z1(k) + cross(k, 0, z):
            cp.start()

    def second(k):
        for cp in z1(k):
            cp.wait_recv()
        for cp in z2(k) + cross(k, 1, zr_i) + cross(k, 2, zl_i):
            cp.start()

    def third(k):
        for cp in z2(k):
            cp.wait_recv()
        for cp in cross(k, 3, zo_i):
            cp.start()

    for k in range(NCH + 3):
        if k < NCH:
            mix(k)
        if 0 <= k - 1 < NCH:
            gathered(k - 1)
        if 0 <= k - 2 < NCH:
            second(k - 2)
        if 0 <= k - 3 < NCH:
            third(k - 3)
    for k in range(NCH):
        for cp in cross(k, 0, z) + cross(k, 1, zr_i) + cross(k, 2, zl_i) + cross(k, 3, zo_i):
            cp.wait_recv()

    @pl.loop(0, 4)
    def _(i):
        rows = pl.ds(pl.multiple_of(i * 256, 256), 256)
        lhs = g[pl.ds(i, 1)].reshape(256, D)
        scores = jnp.dot(lhs, head_w[...], preferred_element_type=F32) + head_b[...] + noise[0, rows, :]
        peak = jnp.max(scores, axis=1, keepdims=True)
        weights = jnp.exp(scores - peak).astype(BF)
        code = jnp.dot(weights, book_x[...], preferred_element_type=F32)
        code = jnp.where(lax.broadcasted_iota(jnp.int32, code.shape, 1) == SIDE + 1, peak, code)
        flipped = jnp.transpose(code)
        turned[:, pl.ds(pl.multiple_of(128 + i * 256, 128), 256)] = flipped[0:MSG, :]

    zeros = jnp.zeros((MSG, 128), F32)
    turned[:, 0:128] = zeros
    turned[:, 1152:1280] = zeros
    cells = turned[...]
    for parity, shift in ((0, 96), (1, 32)):
        rolled = pltpu.roll(cells, 1280 - shift, 1)
        for i in range(8):
            to = 2 * i + parity
            start = (128 + 64 * to - 32 - shift)
            stage[to] = rolled[:, start:start + 128]

    posts = []
    for o in range(1, 16):
        to = (mp + o) % 16
        cp = remote(stage.at[to], got.at[o], m_s.at[o], m_r.at[o], (dp, to))
        cp.start()
        posts.append(cp)
    got[0] = stage[mp]
    for cp in posts:
        cp.wait_recv()
    peaks = got[:, SIDE + 1:SIDE + 2, :]
    factor = jnp.exp(peaks - jnp.max(peaks, axis=0, keepdims=True))
    sums = jnp.sum(got[:, 0:MSG, :] * factor, axis=0)
    lane = lax.broadcasted_iota(jnp.int32, (1, 128), 1)
    outside = jnp.logical_or(jnp.logical_and(mp == 0, lane < 32), jnp.logical_and(mp == 15, lane >= 96))
    soft = jnp.where(outside, 0.0, sums[0:32] / jnp.where(outside, 1.0, sums[32:33]))
    taps = []
    for i in range(3):
        for j in range(3):
            offset = 32 * (i - 1) + (j - 1)
            tap = soft if offset == 0 else pltpu.roll(soft, (-offset) % 128, 1)
            if j == 0:
                tap = jnp.where(lane % 32 == 0, 0.0, tap)
            if j == 2:
                tap = jnp.where(lane % 32 == 31, 0.0, tap)
            taps.append(tap)
    square = lax.broadcasted_iota(jnp.int32, (32, 32), 0) == lax.broadcasted_iota(jnp.int32, (32, 32), 1)
    conv = jnp.sum(jnp.where(square, phi_b[...], 0.0), axis=1, keepdims=True)
    for i in range(3):
        for j in range(3):
            conv = conv + jnp.dot(
                phi[i, j], taps[3 * i + j], preferred_element_type=F32, precision=lax.Precision.HIGHEST
            )
    total = 0.5 * soft + 0.5 * conv
    out[0] = f_hat[0] + pltpu.roll(total, 96, 1)[:, 0:64]

    for cp in t + posts:
        cp.wait_send()
    for k in range(NCH):
        away_copy(k).wait_send()

        @pl.when(jnp.logical_not(same))
        def _():
            home_copy(k).wait_send()

        for cp in z1(k) + z2(k) + cross(k, 0, z) + cross(k, 1, zr_i) + cross(k, 2, zl_i) + cross(k, 3, zo_i):
            cp.wait_send()


NCH = 4
CR = 64 // NCH


def kernel(
    tok, ada, gate, up_w, up_b, down_w, down_b, ada_head, head_w, head_b, noise, book, phi, phi_b, f_hat, out, f_out,
    ffn_scratch, head_scratch, head_w_here, noise_here, load_s,
):
    ylo, x, yhi, z, core = position()
    dp, mp = lax.axis_index("dp"), lax.axis_index("mp")
    arrived = greet(
        [
            device(1 - ylo, x, yhi, z, core), device(1 - ylo, x, 1 - yhi, z, core),
            device(1 - ylo, x, 1 - yhi, z, 1 - core),
            device(ylo, (x + 1) % 4, yhi, z, core), device(ylo, (x + 3) % 4, yhi, z, core),
        ]
        + [(dp, (mp + o) % 16) for o in range(1, 16)]
    )
    loads = [
        pltpu.make_async_copy(head_w, head_w_here, load_s.at[0]),
        pltpu.make_async_copy(noise, noise_here, load_s.at[1]),
    ]
    for cp in loads:
        cp.start()
    book_x = head_scratch[4]
    wide = jnp.concatenate([book[...].astype(F32), jnp.zeros((96, VB), F32)], axis=0)
    wide = jnp.where(lax.broadcasted_iota(jnp.int32, (128, VB), 0) == SIDE, 1.0, wide)
    book_x[...] = jnp.transpose(wide).astype(BF)
    ffn_part(arrived, tok, ada, gate, up_w, up_b, down_w, down_b, out, *ffn_scratch)
    for cp in loads:
        cp.wait()
    head_part(out, ada_head, head_w_here, head_b, noise_here, phi, phi_b, f_hat, f_out, *head_scratch)


def body(
    tokens, ada_ffn, ffn_gate, up_weight, up_bias, down_weight, down_bias, ada_head,
    head_weight, head_bias, gumbel_noise, codebook, phi_weight, phi_bias, f_hat,
):
    dma = pltpu.SemaphoreType.DMA
    widths = [UNITS[k][3] for k in CHUNKS]
    vmem, anywhere = pl.BlockSpec(memory_space=pltpu.VMEM), pl.BlockSpec(memory_space=pl.ANY)
    ffn_scratch = [
        pltpu.VMEM((4, ROWS, D), BF),
        pltpu.VMEM((4 * HID, D), BF),
        [pltpu.VMEM((4 * HID, w), BF) for w in widths],
        pltpu.VMEM((4, 1, HID), F32),
        pltpu.VMEM((1, 4 * HID), F32),
        pltpu.VMEM((512, 4 * HID), BF),
        [pltpu.VMEM((4, ROWS, w), F32) for w in widths],
        [pltpu.VMEM((ROWS, w), BF) for w in widths],
        [pltpu.VMEM((2, 2, 64, w), BF) for w in widths],
        [pltpu.VMEM((2, 3, 64, w), BF) for w in widths],
        dma((3 + NC,)),
        dma((NU,)), dma((NU,)),
        dma((NU, 2)), dma((NU, 2)),
        dma((NU, 2)), dma((NU, 2)),
        dma((NU,)), dma((NU,)),
        dma((1 + NC,)), dma((1 + NC,)),
        dma((4,)), dma((4,)),
        dma((3,)), dma((3,)),
        dma((NC, 2, 2)), dma((NC, 2, 2)),
        dma((NC, 2)), dma((NC, 2)),
    ]
    head_scratch = [
        pltpu.VMEM((ROWS, D), BF),
        pltpu.VMEM((64, D), BF),
        pltpu.VMEM((64, D), BF),
        pltpu.VMEM((4, 2, 2, 64, D), BF),
        pltpu.VMEM((VB, 128), BF),
        pltpu.VMEM((16, MSG, 128), F32),
        pltpu.VMEM((MSG, 1280), F32),
        pltpu.VMEM((16, MSG, 128), F32),
        dma((NCH,)), dma((NCH,)),
        dma((NCH, 2)), dma((NCH, 2)),
        dma((NCH,)),
        dma((NCH, 2, 2)), dma((NCH, 2, 2)),
        dma((NCH, 2)), dma((NCH, 2)),
        dma((NCH, 4, 2)), dma((NCH, 4, 2)),
        dma((16,)), dma((16,)),
    ]
    return pl.pallas_call(
        kernel,
        out_shape=(jax.ShapeDtypeStruct((ROWS, D), BF), jax.ShapeDtypeStruct((1, 32, 64), F32)),
        in_specs=[vmem, vmem, vmem, anywhere, vmem, anywhere, vmem, vmem, anywhere, vmem, anywhere] + [vmem] * 4,
        out_specs=(vmem, vmem),
        scratch_shapes=[
            ffn_scratch,
            head_scratch,
            pltpu.VMEM((D, VB), BF),
            pltpu.VMEM((1, 1024, VB), F32),
            dma((2,)),
        ],
        name="var_step",
        compiler_params=pltpu.CompilerParams(
            collective_id=1, has_side_effects=True, vmem_limit_bytes=60 * 1024 * 1024
        ),
    )(
        tokens, ada_ffn, ffn_gate, up_weight.T, up_bias.reshape(1, -1), down_weight, down_bias.reshape(1, -1),
        ada_head, head_weight, head_bias.reshape(1, -1), gumbel_noise, codebook.T,
        jnp.transpose(phi_weight, (2, 3, 0, 1)), phi_bias.reshape(1, -1), f_hat,
    )


def solution(mesh):
    in_specs = (
        P(("dp", "mp"), None),
        P("dp", None, None),
        P("dp", None),
        P(None, "mp"),
        P("mp"),
        P("mp", None),
        P(),
        P("dp", None, None),
        P(None, "mp"),
        P("mp"),
        P("dp", None, "mp"),
        P("mp", None),
        P(),
        P(),
        P("dp", None, "mp"),
    )
    out_specs = (P(("dp", "mp"), None), P("dp", None, "mp"))
    return jax.shard_map(body, mesh=mesh, in_specs=in_specs, out_specs=out_specs, check_vma=False)
```

time: 152 us -> 129 us (0.85)
  Pallas kernels: 141 us -> 122 us
  local copies, waits for them, and re-layouts: 10.2 us -> 5.82 us
    pallas_call x2 -> x1, Pallas kernels: 141 us -> 122 us  [body(): pl.pallas_call(kernel, out_shape=(jax.ShapeDtypeStruct((ROWS, D), BF), ja...]
    unnamed x16 -> x2, local copies, waits for them, and re-layouts: 7.41 us -> 3.24 us
where the time goes in v2:
time: 129 us; the launch traced here: 128 us
  Pallas kernels  122 us (95%)
  local copies, waits for them, and re-layouts  5.82 us (5%)
    pallas_call x1, Pallas kernels, body(): pl.pallas_call(kernel, out_shape=(jax.ShapeDtypeStruct((ROWS, D), BF), ja...  122 us
    unnamed x2, local copies, waits for them, and re-layouts  3.24 us

profile of v2, /device:TPU:1, one launch (start us, length us, event | category | flops | bytes accessed | tf_op | source)
XLA Modules:
  0.0 128.4 jit_solution(1796420429273579266)
XLA Ops:
  0.6 1.3 reshape.16.up_b
  1.9 1.3 %reshape.17.down_b = f32[1,2304]{1,0:T(1,128)} reshape(f32[2304]{0:T(1024)} %param.21) | data formatting | bytes 18432 | tf_op jit(solution)/shard_map/reshape | solution.py:605
  3.2 121.9 %var_step.1 = (bf16[128,2304]{1,0:T(8,128)(2,1)}, f32[1,32,64]{2,1,0:T(8,128)}) custom-call(bf16[128,2304]{1,0:T(8,128)(2,1)} %tok.1, f32[2,2,2304]{2,1,0:T(2,128)} %ada.1, f32[2,2304]{1,0:T(2,128)} %gate.1, bf16[576,2304]{1,0:T(8,128)(2,1)} %bitcast.5, f32[1,576]{1,0:T(1,128)} %reshape.16.up_b, bf16[576,2304]{1,0:T(8,128)(2,1)} %down_w.1, ...), custom_call_target="tpu_custom_call" | custom-call | tf_op jit(solution)/shard_map/var_step/pallas_call | solution.py:588
  125.1 1.9 %copy.19 = bf16[128,2304]{1,0:T(8,128)(2,1)} copy(bf16[128,2304]{1,0:T(8,128)(2,1)} %get-tuple-element.4) | data formatting | bytes 1179648
  127.0 1.3 %copy.20 = f32[1,32,64]{2,1,0:T(8,128)} copy(f32[1,32,64]{2,1,0:T(8,128)} %get-tuple-element.5) | data formatting | bytes 16384

commit v3 on v2

--- a/solution.py
+++ b/solution.py
@@ -16,6 +16,7 @@
 HID = 576
 FOREIGN = 2 * HID
 DQ = HID // 4
+TH = HID // 2
 UNITS = (
     ("ring", "up", 0, 128),
     ("ring", "up", 128, 192),
@@ -38,8 +39,8 @@
     ("tile", 5), ("tile", 6), ("tile", 7), ("tile", 8), ("a", 4),
     ("first", 0), ("y", 6), ("a", 5), ("second", 0), ("b", 4),
     ("first", 1), ("b", 5), ("finish", 0), ("first", 2), ("a", 6),
-    ("second", 1), ("first", 3), ("second", 2), ("finish", 1), ("second", 3),
-    ("finish", 2), ("finish", 3),
+    ("second", 1), ("first", 3), ("panel", 0), ("second", 2), ("finish", 1),
+    ("panel", 1), ("second", 3), ("finish", 2), ("finish", 3),
 )
 NARROW = 256
 FIRST = 1024
@@ -82,8 +83,8 @@
 
 
 def ffn_part(
-    arrived, tok, ada, gate, up_w, up_b, down_w, down_b, out,
-    xn, up, dns, ub, bias_row, hid, parts, opps, nbrs, gots,
+    arrived, ahead, tok, ada, gate, up_w, up_b, down_w, down_b, out,
+    xn, up, dns, ub, bias_row, down_row, hid, parts, opps, nbrs, gots,
     loc_s, y_s, y_r, a_s, a_r, b_s, b_r, c_s, c_r, o_s, o_r, z_s, z_r, bias_s, bias_r,
     p_s, p_r, q_s, q_r,
 ):
@@ -107,8 +108,10 @@
     loc_dn = [
         pltpu.make_async_copy(down_w.at[:, cols(j)], dns[j].at[own_rows], loc_s.at[3 + j]) for j in range(NC)
     ]
-    loc_bias = pltpu.make_async_copy(up_b, ub.at[0], loc_s.at[2])
+    loc_bias = pltpu.make_async_copy(up_b, ub.at[0, 0], loc_s.at[2])
     loc_bias.start()
+    loc_down = pltpu.make_async_copy(down_b, down_row.at[0], loc_s.at[3 + NC])
+    loc_down.start()
 
     @pl.loop(0, ROWS // 16)
     def _(i):
@@ -177,9 +180,9 @@
         remote(down_w.at[:, cols(j)], dns[j].at[sib_rows], o_s.at[1 + j], o_r.at[1 + j], sib) for j in range(NC)
     ]
     biases = [
-        remote(up_b, ub.at[1], bias_s.at[0], bias_r.at[0], sib),
-        remote(up_b, ub.at[2], bias_s.at[1], bias_r.at[1], partner),
-        remote(up_b, ub.at[3], bias_s.at[2], bias_r.at[2], partner_sib),
+        remote(up_b, ub.at[1, 0], bias_s.at[0], bias_r.at[0], sib),
+        remote(up_b, ub.at[2, 0], bias_s.at[1], bias_r.at[1], partner),
+        remote(up_b, ub.at[3, 0], bias_s.at[2], bias_r.at[2], partner_sib),
     ]
 
     def start(*copies):
@@ -257,7 +260,7 @@
         recv(*ind[j], *p2[j])
         for rows, left, right in ((low, 2, 1), (high, 1, 2)):
             total = parts[j][z, rows] + gots[j][0, left].astype(F32) + gots[j][1, right].astype(F32)
-            total = total + down_b[:, cols(j)]
+            total = total + down_row[:, cols(j)]
             out[rows, cols(j)] = (
                 tok[rows, cols(j)].astype(F32) + gate[pl.ds(yhi, 1), cols(j)] * total
             ).astype(BF)
@@ -274,6 +277,14 @@
             at = PUSHED.index(k)
             if 0 < at < NU - 2:
                 start(y[PUSHED[at + 2]])
+            if k == PUSHED[-1]:
+                start(ahead[0], *ahead[3])
+        elif op == "panel" and k == 0:
+            recv(ahead[0])
+            start(*ahead[1])
+        elif op == "panel":
+            recv(*ahead[1])
+            start(*ahead[2])
         elif op == "a":
             recv(*a[k])
             start(*(b[k] if UNITS[k][0] == "ring" else [c[k]]))
@@ -285,6 +296,7 @@
             start(*z2, *own_dn)
         elif op == "z":
             loc_bias.wait()
+            loc_down.wait()
             recv(*biases)
             bias_row[...] = jnp.concatenate([ub[i] for i in range(4)], axis=1)
             loc_up.wait()
@@ -313,7 +325,7 @@
 
 
 def head_part(
-    blk, ada, head_w, head_b, noise, phi, phi_b, f_hat, out,
+    ahead, blk, ada, head_w, head_b, noise, phi, phi_b, f_hat, out,
     h, mine, theirs, g, book_x, stage, turned, got,
     t_s, t_r, y_s, y_r, l_s, z_s, z_r, w_s, w_r, c_s, c_r, m_s, m_r,
 ):
@@ -345,81 +357,72 @@
     for k in range(NCH):
         normalise(pl.ds(pl.multiple_of(lo + k * CR, CR), CR))
     same = ylo == yhi
-    home = device(yhi, x, yhi, z, core)
-    away = device(yhi, x, 1 - yhi, z, core)
     own_weight = jnp.where(ylo == 0, 1.0 + GUIDE, -GUIDE)
     twin_weight = jnp.where(ylo == 0, -GUIDE, 1.0 + GUIDE)
 
-    def slot(k, zi, half):
-        return g.at[zi, core, half, pl.ds(k * CR, CR)]
-
-    def away_copy(k):
-        return remote(mine.at[pl.ds(k * CR, CR)], slot(k, z, ylo), y_s.at[k, 0], y_r.at[k, ylo], away)
-
-    def home_copy(k):
-        return remote(mine.at[pl.ds(k * CR, CR)], slot(k, z, ylo), y_s.at[k, 1], y_r.at[k, ylo], home)
-
-    def stay_copy(k):
-        return pltpu.make_async_copy(mine.at[pl.ds(k * CR, CR)], slot(k, z, ylo), l_s.at[k])
-
-    def z1(k):
-        return [
-            remote(slot(k, z, i), slot(k, z, i), z_s.at[k, d, i], z_r.at[k, d, i], target)
-            for d, target in ((0, zr), (1, zl)) for i in range(2)
+    def slot(k, zi):
+        return g.at[zi, core, pl.ds(k * CR, CR)]
+
+    def slot_half(k, zi, half):
+        return g.at[zi, core, pl.ds(k * CR, CR), pl.ds(half * (D // 2), D // 2)]
+
+    def mixed(k):
+        return mine.at[pl.ds(k * CR, CR)]
+
+    swap = [remote(mixed(k), slot(k, z), y_s.at[k], y_r.at[k], partner) for k in range(NCH)]
+    stay = [pltpu.make_async_copy(mixed(k), slot(k, z), l_s.at[k]) for k in range(NCH)]
+    z1 = [
+        [remote(slot(k, z), slot(k, z), z_s.at[k, d], z_r.at[k, d], to) for d, to in ((0, zr), (1, zl))]
+        for k in range(NCH)
+    ]
+    z2 = [
+        [
+            remote(slot_half(k, zl_i, 0), slot_half(k, zl_i, 0), w_s.at[k, 0], w_r.at[k, 0], zr),
+            remote(slot_half(k, zr_i, 1), slot_half(k, zr_i, 1), w_s.at[k, 1], w_r.at[k, 1], zl),
         ]
-
-    def z2(k):
-        return [
-            remote(slot(k, zl_i, 0), slot(k, zl_i, 0), w_s.at[k, 0], w_r.at[k, 0], zr),
-            remote(slot(k, zr_i, 1), slot(k, zr_i, 1), w_s.at[k, 1], w_r.at[k, 1], zl),
-        ]
-
-    def cross(k, step, zi):
-        return [
-            remote(slot(k, zi, i), slot(k, zi, i), c_s.at[k, step, i], c_r.at[k, step, i], sib)
-            for i in range(2)
-        ]
+        for k in range(NCH)
+    ]
+    cross = [
+        [remote(slot(k, zi), slot(k, zi), c_s.at[k, i], c_r.at[k, i], sib) for i, zi in enumerate((z, zr_i, zl_i, zo_i))]
+        for k in range(NCH)
+    ]
 
     def mix(k):
         t[k].wait_recv()
         rows = pl.ds(k * CR, CR)
         own = h[pl.ds(pl.multiple_of(lo + k * CR, CR), CR), :].astype(F32)
         mine[rows, :] = (own_weight * own + twin_weight * theirs[rows, :].astype(F32)).astype(BF)
-        away_copy(k).start()
 
         @pl.when(same)
         def _():
-            stay_copy(k).start()
+            stay[k].start()
 
         @pl.when(jnp.logical_not(same))
         def _():
-            home_copy(k).start()
+            swap[k].start()
 
     def gathered(k):
         @pl.when(same)
         def _():
-            stay_copy(k).wait()
-            remote(mine.at[pl.ds(k * CR, CR)], slot(k, z, 1 - ylo), y_s.at[k, 0], y_r.at[k, 1 - ylo], away).wait_recv()
+            stay[k].wait()
 
         @pl.when(jnp.logical_not(same))
         def _():
-            for i in range(2):
-                remote(mine.at[pl.ds(k * CR, CR)], slot(k, z, i), y_s.at[k, 0], y_r.at[k, i], away).wait_recv()
-
-        for cp in z1(k) + cross(k, 0, z):
+            swap[k].wait_recv()
+
+        for cp in z1[k] + cross[k][:1]:
             cp.start()
 
     def second(k):
-        for cp in z1(k):
+        for cp in z1[k]:
             cp.wait_recv()
-        for cp in z2(k) + cross(k, 1, zr_i) + cross(k, 2, zl_i):
+        for cp in z2[k] + cross[k][1:3]:
             cp.start()
 
     def third(k):
-        for cp in z2(k):
+        for cp in z2[k]:
             cp.wait_recv()
-        for cp in cross(k, 3, zo_i):
-            cp.start()
+        cross[k][3].start()
 
     for k in range(NCH + 3):
         if k < NCH:
@@ -430,21 +433,35 @@
             second(k - 2)
         if 0 <= k - 3 < NCH:
             third(k - 3)
+    for cp in ahead[2] + ahead[3]:
+        cp.wait_recv()
     for k in range(NCH):
-        for cp in cross(k, 0, z) + cross(k, 1, zr_i) + cross(k, 2, zl_i) + cross(k, 3, zo_i):
+        for cp in cross[k]:
             cp.wait_recv()
 
-    @pl.loop(0, 4)
+    column = lax.broadcasted_iota(jnp.int32, (4, 64, 128), 2)
+    nothing = jnp.where(column == SIDE + 1, -1e30, 0.0)
+
+    @pl.loop(0, 2)
     def _(i):
-        rows = pl.ds(pl.multiple_of(i * 256, 256), 256)
-        lhs = g[pl.ds(i, 1)].reshape(256, D)
-        scores = jnp.dot(lhs, head_w[...], preferred_element_type=F32) + head_b[...] + noise[0, rows, :]
-        peak = jnp.max(scores, axis=1, keepdims=True)
-        weights = jnp.exp(scores - peak).astype(BF)
-        code = jnp.dot(weights, book_x[...], preferred_element_type=F32)
-        code = jnp.where(lax.broadcasted_iota(jnp.int32, code.shape, 1) == SIDE + 1, peak, code)
-        flipped = jnp.transpose(code)
-        turned[:, pl.ds(pl.multiple_of(128 + i * 256, 128), 256)] = flipped[0:MSG, :]
+        lhs = g[pl.ds(2 * i, 2)].reshape(256, D)
+        scores = []
+        for p in range(2):
+            logits = jnp.dot(lhs, head_w[p], preferred_element_type=F32) + head_b[p]
+            scores.append(logits + noise[p, pl.ds(4 * i, 4)].reshape(256, VB))
+        peak = jnp.maximum(
+            jnp.max(scores[0], axis=1, keepdims=True), jnp.max(scores[1], axis=1, keepdims=True)
+        )
+        code = jnp.zeros((256, 128), F32)
+        for p in range(2):
+            weights = jnp.exp(scores[p] - peak).astype(BF)
+            code = code + jnp.dot(weights, book_x[p], preferred_element_type=F32)
+        code = jnp.where(lax.broadcasted_iota(jnp.int32, code.shape, 1) == SIDE + 1, peak, code).reshape(4, 64, 128)
+        spread = jnp.concatenate(
+            [jnp.where(yhi == 0, code, nothing), jnp.where(yhi == 1, code, nothing)], axis=1
+        ).reshape(512, 128)
+        flipped = jnp.transpose(spread)
+        turned[:, pl.ds(pl.multiple_of(128 + i * 512, 128), 512)] = flipped[0:MSG, :]
 
     zeros = jnp.zeros((MSG, 128), F32)
     turned[:, 0:128] = zeros
@@ -495,13 +512,12 @@
     for cp in t + posts:
         cp.wait_send()
     for k in range(NCH):
-        away_copy(k).wait_send()
 
         @pl.when(jnp.logical_not(same))
         def _():
-            home_copy(k).wait_send()
-
-        for cp in z1(k) + z2(k) + cross(k, 0, z) + cross(k, 1, zr_i) + cross(k, 2, zl_i) + cross(k, 3, zo_i):
+            swap[k].wait_send()
+
+        for cp in z1[k] + z2[k] + cross[k]:
             cp.wait_send()
 
 
@@ -511,7 +527,7 @@
 
 def kernel(
     tok, ada, gate, up_w, up_b, down_w, down_b, ada_head, head_w, head_b, noise, book, phi, phi_b, f_hat, out, f_out,
-    ffn_scratch, head_scratch, head_w_here, noise_here, load_s,
+    ffn_scratch, head_scratch, head_w_here, head_b_here, noise_here, load_s, far_s, far_r, panel_s, panel_r,
 ):
     ylo, x, yhi, z, core = position()
     dp, mp = lax.axis_index("dp"), lax.axis_index("mp")
@@ -523,20 +539,66 @@
         ]
         + [(dp, (mp + o) % 16) for o in range(1, 16)]
     )
+    far = (dp, (mp + 8) % 16)
+    mine_rows = pl.ds(pl.multiple_of(yhi * 64, 64), 64)
+    far_rows = pl.ds(pl.multiple_of((1 - yhi) * 64, 64), 64)
     loads = [
-        pltpu.make_async_copy(head_w, head_w_here, load_s.at[0]),
-        pltpu.make_async_copy(noise, noise_here, load_s.at[1]),
+        pltpu.make_async_copy(head_w, head_w_here.at[0], load_s.at[0]),
+        pltpu.make_async_copy(noise.at[:, mine_rows], noise_here.at[0], load_s.at[1]),
+        pltpu.make_async_copy(head_b, head_b_here.at[0], load_s.at[2]),
     ]
     for cp in loads:
         cp.start()
     book_x = head_scratch[4]
     wide = jnp.concatenate([book[...].astype(F32), jnp.zeros((96, VB), F32)], axis=0)
     wide = jnp.where(lax.broadcasted_iota(jnp.int32, (128, VB), 0) == SIDE, 1.0, wide)
-    book_x[...] = jnp.transpose(wide).astype(BF)
-    ffn_part(arrived, tok, ada, gate, up_w, up_b, down_w, down_b, out, *ffn_scratch)
+    book_x[0] = jnp.transpose(wide).astype(BF)
+    def quarter(ref, index, first=0, count=HID):
+        return ref.at[pl.ds(pl.multiple_of(index * HID + first, 16), count)]
+
+    there = head_w_here.at[1]
+    x_l, x_r = (x + 3) % 4, (x + 1) % 4
+    ways = ((0, device(ylo, x_r, yhi, z, core), x_l), (1, device(ylo, x_l, yhi, z, core), x_r))
+    ahead = [
+        remote(quarter(head_w, x), quarter(there, x), far_s.at[0], far_r.at[0], far),
+        [remote(quarter(there, x), quarter(there, x), panel_s.at[0, d], panel_r.at[0, d], to) for d, to, _ in ways],
+        [
+            remote(
+                quarter(there, back, d * TH, TH), quarter(there, back, d * TH, TH),
+                panel_s.at[1, d], panel_r.at[1, d], to,
+            )
+            for d, to, back in ways
+        ],
+        [
+            remote(noise.at[:, far_rows], noise_here.at[1], far_s.at[1], far_r.at[1], far),
+            remote(book_x.at[0], book_x.at[1], far_s.at[2], far_r.at[2], far),
+            remote(head_b, head_b_here.at[1], far_s.at[3], far_r.at[3], far),
+        ],
+    ]
+    ffn_part(arrived, ahead, tok, ada, gate, up_w, up_b, down_w, down_b, out, *ffn_scratch)
     for cp in loads:
         cp.wait()
-    head_part(out, ada_head, head_w_here, head_b, noise_here, phi, phi_b, f_hat, f_out, *head_scratch)
+    head_part(
+        ahead, out, ada_head, head_w_here, head_b_here, noise_here, phi, phi_b, f_hat, f_out, *head_scratch
+    )
+    for cp in ahead[:1] + ahead[1] + ahead[2] + ahead[3]:
+        cp.wait_send()
+
+
+def deliver_kernel(rows, cells, rows_out, cells_out):
+    rows_out[...] = rows[...]
+    cells_out[...] = cells[...]
+
+
+def deliver(rows, cells):
+    vmem = pl.BlockSpec(memory_space=pltpu.VMEM)
+    return pl.pallas_call(
+        deliver_kernel,
+        out_shape=tuple(jax.ShapeDtypeStruct(v.shape, v.dtype) for v in (rows, cells)),
+        in_specs=[vmem] * 2,
+        out_specs=(vmem, vmem),
+        name="deliver",
+    )(rows, cells)
 
 
 def body(
@@ -552,12 +614,13 @@
         [pltpu.VMEM((4 * HID, w), BF) for w in widths],
         pltpu.VMEM((4, 1, HID), F32),
         pltpu.VMEM((1, 4 * HID), F32),
+        pltpu.VMEM((1, D), F32),
         pltpu.VMEM((512, 4 * HID), BF),
         [pltpu.VMEM((4, ROWS, w), F32) for w in widths],
         [pltpu.VMEM((ROWS, w), BF) for w in widths],
         [pltpu.VMEM((2, 2, 64, w), BF) for w in widths],
         [pltpu.VMEM((2, 3, 64, w), BF) for w in widths],
-        dma((3 + NC,)),
+        dma((4 + NC,)),
         dma((NU,)), dma((NU,)),
         dma((NU, 2)), dma((NU, 2)),
         dma((NU, 2)), dma((NU, 2)),
@@ -572,40 +635,44 @@
         pltpu.VMEM((ROWS, D), BF),
         pltpu.VMEM((64, D), BF),
         pltpu.VMEM((64, D), BF),
-        pltpu.VMEM((4, 2, 2, 64, D), BF),
-        pltpu.VMEM((VB, 128), BF),
+        pltpu.VMEM((4, 2, 64, D), BF),
+        pltpu.VMEM((2, VB, 128), BF),
         pltpu.VMEM((16, MSG, 128), F32),
         pltpu.VMEM((MSG, 1280), F32),
         pltpu.VMEM((16, MSG, 128), F32),
         dma((NCH,)), dma((NCH,)),
+        dma((NCH,)), dma((NCH,)),
+        dma((NCH,)),
         dma((NCH, 2)), dma((NCH, 2)),
-        dma((NCH,)),
-        dma((NCH, 2, 2)), dma((NCH, 2, 2)),
         dma((NCH, 2)), dma((NCH, 2)),
-        dma((NCH, 4, 2)), dma((NCH, 4, 2)),
+        dma((NCH, 4)), dma((NCH, 4)),
         dma((16,)), dma((16,)),
     ]
-    return pl.pallas_call(
+    rows, cells = pl.pallas_call(
         kernel,
         out_shape=(jax.ShapeDtypeStruct((ROWS, D), BF), jax.ShapeDtypeStruct((1, 32, 64), F32)),
-        in_specs=[vmem, vmem, vmem, anywhere, vmem, anywhere, vmem, vmem, anywhere, vmem, anywhere] + [vmem] * 4,
+        in_specs=[vmem, vmem, vmem, anywhere, anywhere, anywhere, anywhere, vmem, anywhere, vmem, anywhere] + [vmem] * 4,
         out_specs=(vmem, vmem),
         scratch_shapes=[
             ffn_scratch,
             head_scratch,
-            pltpu.VMEM((D, VB), BF),
-            pltpu.VMEM((1, 1024, VB), F32),
-            dma((2,)),
+            pltpu.VMEM((2, D, VB), BF),
+            pltpu.VMEM((2, 1, VB), F32),
+            pltpu.VMEM((2, 8, 64, VB), F32),
+            dma((3,)),
+            dma((4,)), dma((4,)),
+            dma((2, 2)), dma((2, 2)),
         ],
         name="var_step",
         compiler_params=pltpu.CompilerParams(
             collective_id=1, has_side_effects=True, vmem_limit_bytes=60 * 1024 * 1024
         ),
     )(
-        tokens, ada_ffn, ffn_gate, up_weight.T, up_bias.reshape(1, -1), down_weight, down_bias.reshape(1, -1),
-        ada_head, head_weight, head_bias.reshape(1, -1), gumbel_noise, codebook.T,
+        tokens, ada_ffn, ffn_gate, up_weight.T, up_bias, down_weight, down_bias,
+        ada_head, head_weight, head_bias.reshape(1, -1), gumbel_noise.reshape(8, 128, VB), codebook.T,
         jnp.transpose(phi_weight, (2, 3, 0, 1)), phi_bias.reshape(1, -1), f_hat,
     )
+    return deliver(rows, cells)
 
 
 def solution(mesh):

time: 129 us -> 117 us (0.907)
  local copies, waits for them, and re-layouts: 5.82 us -> 0 us
  Pallas kernels: 122 us -> 117 us
    pallas_call x1, Pallas kernels: 122 us -> 115 us  [body(): pl.pallas_call(kernel, out_shape=(jax.ShapeDtypeStruct((ROWS, D), BF), ja...]
    unnamed x2 -> x0, local copies, waits for them, and re-layouts: 3.24 us -> none
    reshape x2 -> x0, local copies, waits for them, and re-layouts: 2.58 us -> none  [the longest x1 1.31 us: body(): down_bias.reshape(1, -1)]
    pallas_call x0 -> x1, Pallas kernels: none -> 1.92 us  [deliver(): pl.pallas_call(deliver_kernel, out_shape=tuple((jax.ShapeDtypeStruct(v.sh...]
where the time goes in v3:
time: 117 us
  Pallas kernels  117 us (100%)
    pallas_call x1, Pallas kernels, body(): pl.pallas_call(kernel, out_shape=(jax.ShapeDtypeStruct((ROWS, D), BF), ja...  115 us

profile of v3, /device:TPU:1, one launch (start us, length us, event | category | flops | bytes accessed | tf_op | source)
XLA Modules:
  0.0 117.2 jit_solution(5473351277123316193)
XLA Ops:
  0.6 114.6 %var_step.1 = (bf16[128,2304]{1,0:T(8,128)(2,1)}, f32[1,32,64]{2,1,0:T(8,128)}) custom-call(bf16[128,2304]{1,0:T(8,128)(2,1)} %tok.1, f32[2,2,2304]{2,1,0:T(2,128)} %ada.1, f32[2,2304]{1,0:T(2,128)} %gate.1, bf16[576,2304]{1,0:T(8,128)(2,1)} %bitcast.6, f32[576]{0:T(1024)} %up_b.1, bf16[576,2304]{1,0:T(8,128)(2,1)} %down_w.1, f32[2304]{0:T(1024)} %down_b.1, ...), custom_call_target="tpu_custom_call" | custom-call | tf_op jit(solution)/shard_map/var_step/pallas_call | solution.py:651
  115.3 1.9 %deliver.1 = (bf16[128,2304]{1,0:T(8,128)(2,1)}, f32[1,32,64]{2,1,0:T(8,128)}) custom-call(bf16[128,2304]{1,0:T(8,128)(2,1)} %get-tuple-element.4.rows, f32[1,32,64]{2,1,0:T(8,128)} %get-tuple-element.5.cells), custom_call_target="tpu_custom_call" | custom-call | tf_op jit(solution)/shard_map/deliver/pallas_call | solution.py:595

commit v4 on v3

--- a/solution.py
+++ b/solution.py
@@ -39,8 +39,8 @@
     ("tile", 5), ("tile", 6), ("tile", 7), ("tile", 8), ("a", 4),
     ("first", 0), ("y", 6), ("a", 5), ("second", 0), ("b", 4),
     ("first", 1), ("b", 5), ("finish", 0), ("first", 2), ("a", 6),
-    ("second", 1), ("first", 3), ("panel", 0), ("second", 2), ("finish", 1),
-    ("panel", 1), ("second", 3), ("finish", 2), ("finish", 3),
+    ("second", 1), ("first", 3), ("second", 2), ("panel", 0), ("finish", 1),
+    ("second", 3), ("finish", 2), ("finish", 3), ("panel", 1),
 )
 NARROW = 256
 FIRST = 1024

time: 117 us -> 114 us (0.974)
  Pallas kernels: 117 us -> 114 us
    pallas_call x1, Pallas kernels: 115 us -> 112 us  [body(): pl.pallas_call(kernel, out_shape=(jax.ShapeDtypeStruct((ROWS, D), BF), ja...]
where the time goes in v4:
time: 114 us
  Pallas kernels  114 us (100%)
    pallas_call x1, Pallas kernels, body(): pl.pallas_call(kernel, out_shape=(jax.ShapeDtypeStruct((ROWS, D), BF), ja...  112 us

profile of v4, /device:TPU:1, one launch (start us, length us, event | category | flops | bytes accessed | tf_op | source)
XLA Modules:
  0.0 114.2 jit_solution(5230360001884230555)
XLA Ops:
  0.6 111.6 %var_step.1 = (bf16[128,2304]{1,0:T(8,128)(2,1)}, f32[1,32,64]{2,1,0:T(8,128)}) custom-call(bf16[128,2304]{1,0:T(8,128)(2,1)} %tok.1, f32[2,2,2304]{2,1,0:T(2,128)} %ada.1, f32[2,2304]{1,0:T(2,128)} %gate.1, bf16[576,2304]{1,0:T(8,128)(2,1)} %bitcast.6, f32[576]{0:T(1024)} %up_b.1, bf16[576,2304]{1,0:T(8,128)(2,1)} %down_w.1, f32[2304]{0:T(1024)} %down_b.1, ...), custom_call_target="tpu_custom_call" | custom-call | tf_op jit(solution)/shard_map/var_step/pallas_call | solution.py:651
  112.3 1.9 %deliver.1 = (bf16[128,2304]{1,0:T(8,128)(2,1)}, f32[1,32,64]{2,1,0:T(8,128)}) custom-call(bf16[128,2304]{1,0:T(8,128)(2,1)} %get-tuple-element.4.rows, f32[1,32,64]{2,1,0:T(8,128)} %get-tuple-element.5.cells), custom_call_target="tpu_custom_call" | custom-call | tf_op jit(solution)/shard_map/deliver/pallas_call | solution.py:595

commit v5 on v4

--- a/solution.py
+++ b/solution.py
@@ -347,15 +347,13 @@
     ]
     pair = ada[yhi]
 
-    def normalise(rows):
+    for first in (other, lo):
+        rows = pl.ds(first, 64)
         v = norm_rows(blk[rows, :].astype(F32)) * (1.0 + pair[1:2, :]) + pair[0:1, :]
         h[rows, :] = v.astype(BF)
-
-    for k in range(NCH):
-        normalise(pl.ds(pl.multiple_of(other + k * CR, CR), CR))
-        t[k].start()
-    for k in range(NCH):
-        normalise(pl.ds(pl.multiple_of(lo + k * CR, CR), CR))
+        if first is other:
+            for cp in t:
+                cp.start()
     same = ylo == yhi
     own_weight = jnp.where(ylo == 0, 1.0 + GUIDE, -GUIDE)
     twin_weight = jnp.where(ylo == 0, -GUIDE, 1.0 + GUIDE)
@@ -431,19 +429,18 @@
             gathered(k - 1)
         if 0 <= k - 2 < NCH:
             second(k - 2)
-        if 0 <= k - 3 < NCH:
+        if 0 <= k - 3 < NCH - 1:
             third(k - 3)
     for cp in ahead[2] + ahead[3]:
         cp.wait_recv()
     for k in range(NCH):
-        for cp in cross[k]:
+        for cp in cross[k][:3]:
             cp.wait_recv()
 
     column = lax.broadcasted_iota(jnp.int32, (4, 64, 128), 2)
     nothing = jnp.where(column == SIDE + 1, -1e30, 0.0)
 
-    @pl.loop(0, 2)
-    def _(i):
+    def sample(i):
         lhs = g[pl.ds(2 * i, 2)].reshape(256, D)
         scores = []
         for p in range(2):
@@ -462,6 +459,12 @@
         ).reshape(512, 128)
         flipped = jnp.transpose(spread)
         turned[:, pl.ds(pl.multiple_of(128 + i * 512, 128), 512)] = flipped[0:MSG, :]
+
+    sample(z // 2)
+    third(NCH - 1)
+    for k in range(NCH):
+        cross[k][3].wait_recv()
+    sample(1 - z // 2)
 
     zeros = jnp.zeros((MSG, 128), F32)
     turned[:, 0:128] = zeros
@@ -500,12 +503,9 @@
                 tap = jnp.where(lane % 32 == 31, 0.0, tap)
             taps.append(tap)
     square = lax.broadcasted_iota(jnp.int32, (32, 32), 0) == lax.broadcasted_iota(jnp.int32, (32, 32), 1)
-    conv = jnp.sum(jnp.where(square, phi_b[...], 0.0), axis=1, keepdims=True)
-    for i in range(3):
-        for j in range(3):
-            conv = conv + jnp.dot(
-                phi[i, j], taps[3 * i + j], preferred_element_type=F32, precision=lax.Precision.HIGHEST
-            )
+    conv = jnp.sum(jnp.where(square, phi_b[...], 0.0), axis=1, keepdims=True) + jnp.dot(
+        phi[...], jnp.concatenate(taps, axis=0), preferred_element_type=F32, precision=lax.Precision.HIGHEST
+    )
     total = 0.5 * soft + 0.5 * conv
     out[0] = f_hat[0] + pltpu.roll(total, 96, 1)[:, 0:64]
 
@@ -527,7 +527,7 @@
 
 def kernel(
     tok, ada, gate, up_w, up_b, down_w, down_b, ada_head, head_w, head_b, noise, book, phi, phi_b, f_hat, out, f_out,
-    ffn_scratch, head_scratch, head_w_here, head_b_here, noise_here, load_s, far_s, far_r, panel_s, panel_r,
+    ffn_scratch, head_scratch, head_w_here, head_b_here, noise_here, load_s, far_s, far_r, panel_s, panel_r, phi_flat,
 ):
     ylo, x, yhi, z, core = position()
     dp, mp = lax.axis_index("dp"), lax.axis_index("mp")
@@ -549,6 +549,7 @@
     ]
     for cp in loads:
         cp.start()
+    phi_flat[...] = jnp.concatenate([phi[i, j] for i in range(3) for j in range(3)], axis=1)
     book_x = head_scratch[4]
     wide = jnp.concatenate([book[...].astype(F32), jnp.zeros((96, VB), F32)], axis=0)
     wide = jnp.where(lax.broadcasted_iota(jnp.int32, (128, VB), 0) == SIDE, 1.0, wide)
@@ -579,7 +580,7 @@
     for cp in loads:
         cp.wait()
     head_part(
-        ahead, out, ada_head, head_w_here, head_b_here, noise_here, phi, phi_b, f_hat, f_out, *head_scratch
+        ahead, out, ada_head, head_w_here, head_b_here, noise_here, phi_flat, phi_b, f_hat, f_out, *head_scratch
     )
     for cp in ahead[:1] + ahead[1] + ahead[2] + ahead[3]:
         cp.wait_send()
@@ -662,6 +663,7 @@
             dma((3,)),
             dma((4,)), dma((4,)),
             dma((2, 2)), dma((2, 2)),
+            pltpu.VMEM((32, 288), F32),
         ],
         name="var_step",
         compiler_params=pltpu.CompilerParams(

time: 114 us -> 113 us (level)
  no operation moved by 1% of the time
where the time goes in v5:
time: 113 us
  Pallas kernels  113 us (100%)
    pallas_call x1, Pallas kernels, body(): pl.pallas_call(kernel, out_shape=(jax.ShapeDtypeStruct((ROWS, D), BF), ja...  111 us

profile of v5, /device:TPU:1, one launch (start us, length us, event | category | flops | bytes accessed | tf_op | source)
XLA Modules:
  0.0 113.3 jit_solution(16717627739823980990)
XLA Ops:
  0.6 110.7 %var_step.1 = (bf16[128,2304]{1,0:T(8,128)(2,1)}, f32[1,32,64]{2,1,0:T(8,128)}) custom-call(bf16[128,2304]{1,0:T(8,128)(2,1)} %tok.1, f32[2,2,2304]{2,1,0:T(2,128)} %ada.1, f32[2,2304]{1,0:T(2,128)} %gate.1, bf16[576,2304]{1,0:T(8,128)(2,1)} %bitcast.6, f32[576]{0:T(1024)} %up_b.1, bf16[576,2304]{1,0:T(8,128)(2,1)} %down_w.1, f32[2304]{0:T(1024)} %down_b.1, ...), custom_call_target="tpu_custom_call" | custom-call | tf_op jit(solution)/shard_map/var_step/pallas_call | solution.py:652
  111.4 1.9 %deliver.1 = (bf16[128,2304]{1,0:T(8,128)(2,1)}, f32[1,32,64]{2,1,0:T(8,128)}) custom-call(bf16[128,2304]{1,0:T(8,128)(2,1)} %get-tuple-element.4.rows, f32[1,32,64]{2,1,0:T(8,128)} %get-tuple-element.5.cells), custom_call_target="tpu_custom_call" | custom-call | tf_op jit(solution)/shard_map/deliver/pallas_call | solution.py:596

commit v6 on v5

--- a/solution.py
+++ b/solution.py
@@ -83,7 +83,7 @@
 
 
 def ffn_part(
-    arrived, ahead, tok, ada, gate, up_w, up_b, down_w, down_b, out,
+    arrived, prepare, ahead, tok, ada, gate, up_w, up_b, down_w, down_b, out,
     xn, up, dns, ub, bias_row, down_row, hid, parts, opps, nbrs, gots,
     loc_s, y_s, y_r, a_s, a_r, b_s, b_r, c_s, c_r, o_s, o_r, z_s, z_r, bias_s, bias_r,
     p_s, p_r, q_s, q_r,
@@ -112,13 +112,6 @@
     loc_bias.start()
     loc_down = pltpu.make_async_copy(down_b, down_row.at[0], loc_s.at[3 + NC])
     loc_down.start()
-
-    @pl.loop(0, ROWS // 16)
-    def _(i):
-        rows = pl.ds(pl.multiple_of(i * 16, 16), 16)
-        pair = ada[yhi]
-        v = norm_rows(tok[rows, :].astype(F32)) * (1.0 + pair[1:2, :]) + pair[0:1, :]
-        xn[z, rows, :] = v.astype(BF)
 
     arrived()
 
@@ -265,7 +258,12 @@
                 tok[rows, cols(j)].astype(F32) + gate[pl.ds(yhi, 1), cols(j)] * total
             ).astype(BF)
 
-    start(y[PUSHED[0]], *z1, *biases, own_up)
+    start(y[PUSHED[0]])
+    pair = ada[yhi]
+    for rows in (low, high):
+        v = norm_rows(tok[rows, :].astype(F32)) * (1.0 + pair[1:2, :]) + pair[0:1, :]
+        xn[z, rows, :] = v.astype(BF)
+    start(*z1, *biases, own_up)
     for cp in loc_dn:
         cp.start()
     y[PUSHED[0]].wait_send()
@@ -294,6 +292,7 @@
         elif op == "z" and k == 1:
             recv(*z1)
             start(*z2, *own_dn)
+            prepare()
         elif op == "z":
             loc_bias.wait()
             loc_down.wait()
@@ -549,11 +548,14 @@
     ]
     for cp in loads:
         cp.start()
-    phi_flat[...] = jnp.concatenate([phi[i, j] for i in range(3) for j in range(3)], axis=1)
     book_x = head_scratch[4]
-    wide = jnp.concatenate([book[...].astype(F32), jnp.zeros((96, VB), F32)], axis=0)
-    wide = jnp.where(lax.broadcasted_iota(jnp.int32, (128, VB), 0) == SIDE, 1.0, wide)
-    book_x[0] = jnp.transpose(wide).astype(BF)
+
+    def prepare():
+        phi_flat[...] = jnp.concatenate([phi[i, j] for i in range(3) for j in range(3)], axis=1)
+        wide = jnp.concatenate([book[...].astype(F32), jnp.zeros((96, VB), F32)], axis=0)
+        wide = jnp.where(lax.broadcasted_iota(jnp.int32, (128, VB), 0) == SIDE, 1.0, wide)
+        book_x[0] = jnp.transpose(wide).astype(BF)
+
     def quarter(ref, index, first=0, count=HID):
         return ref.at[pl.ds(pl.multiple_of(index * HID + first, 16), count)]
 
@@ -576,7 +578,7 @@
             remote(head_b, head_b_here.at[1], far_s.at[3], far_r.at[3], far),
         ],
     ]
-    ffn_part(arrived, ahead, tok, ada, gate, up_w, up_b, down_w, down_b, out, *ffn_scratch)
+    ffn_part(arrived, prepare, ahead, tok, ada, gate, up_w, up_b, down_w, down_b, out, *ffn_scratch)
     for cp in loads:
         cp.wait()
     head_part(

time: 113 us -> 114 us (level)
  no operation moved by 1% of the time
where the time goes in v6:
time: 114 us
  Pallas kernels  113 us (99%)
    pallas_call x1, Pallas kernels, body(): pl.pallas_call(kernel, out_shape=(jax.ShapeDtypeStruct((ROWS, D), BF), ja...  111 us

profile of v6, /device:TPU:1, one launch (start us, length us, event | category | flops | bytes accessed | tf_op | source)
XLA Modules:
  0.0 113.9 jit_solution(411659033814390944)
XLA Ops:
  0.6 111.3 %var_step.1 = (bf16[128,2304]{1,0:T(8,128)(2,1)}, f32[1,32,64]{2,1,0:T(8,128)}) custom-call(bf16[128,2304]{1,0:T(8,128)(2,1)} %tok.1, f32[2,2,2304]{2,1,0:T(2,128)} %ada.1, f32[2,2304]{1,0:T(2,128)} %gate.1, bf16[576,2304]{1,0:T(8,128)(2,1)} %bitcast.6, f32[576]{0:T(1024)} %up_b.1, bf16[576,2304]{1,0:T(8,128)(2,1)} %down_w.1, f32[2304]{0:T(1024)} %down_b.1, ...), custom_call_target="tpu_custom_call" | custom-call | tf_op jit(solution)/shard_map/var_step/pallas_call | solution.py:654
  111.9 1.9 %deliver.1 = (bf16[128,2304]{1,0:T(8,128)(2,1)}, f32[1,32,64]{2,1,0:T(8,128)}) custom-call(bf16[128,2304]{1,0:T(8,128)(2,1)} %get-tuple-element.4.rows, f32[1,32,64]{2,1,0:T(8,128)} %get-tuple-element.5.cells), custom_call_target="tpu_custom_call" | custom-call | tf_op jit(solution)/shard_map/deliver/pallas_call | solution.py:598

commit v7 on v5

--- a/solution.py
+++ b/solution.py
@@ -269,14 +269,14 @@
     for cp in loc_dn:
         cp.start()
     y[PUSHED[0]].wait_send()
-    start(y[PUSHED[1]], y[PUSHED[2]])
+    start(y[PUSHED[1]], y[PUSHED[2]], y[PUSHED[3]])
     for op, k in STEPS:
         if op == "y":
             recv(y[k])
             start(*a[k])
             at = PUSHED.index(k)
-            if 0 < at < NU - 2:
-                start(y[PUSHED[at + 2]])
+            if 0 < at < NU - 3:
+                start(y[PUSHED[at + 3]])
             if k == PUSHED[-1]:
                 start(ahead[0], *ahead[3])
         elif op == "panel" and k == 0:

time: 113 us -> 113 us (level)
  no operation moved by 1% of the time
where the time goes in v7:
time: 113 us
  Pallas kernels  113 us (100%)
    pallas_call x1, Pallas kernels, body(): pl.pallas_call(kernel, out_shape=(jax.ShapeDtypeStruct((ROWS, D), BF), ja...  111 us

profile of v7, /device:TPU:1, one launch (start us, length us, event | category | flops | bytes accessed | tf_op | source)
XLA Modules:
  0.0 113.3 jit_solution(9414243793547644022)
XLA Ops:
  0.6 110.7 %var_step.1 = (bf16[128,2304]{1,0:T(8,128)(2,1)}, f32[1,32,64]{2,1,0:T(8,128)}) custom-call(bf16[128,2304]{1,0:T(8,128)(2,1)} %tok.1, f32[2,2,2304]{2,1,0:T(2,128)} %ada.1, f32[2,2304]{1,0:T(2,128)} %gate.1, bf16[576,2304]{1,0:T(8,128)(2,1)} %bitcast.6, f32[576]{0:T(1024)} %up_b.1, bf16[576,2304]{1,0:T(8,128)(2,1)} %down_w.1, f32[2304]{0:T(1024)} %down_b.1, ...), custom_call_target="tpu_custom_call" | custom-call | tf_op jit(solution)/shard_map/var_step/pallas_call | solution.py:652
  111.4 1.9 %deliver.1 = (bf16[128,2304]{1,0:T(8,128)(2,1)}, f32[1,32,64]{2,1,0:T(8,128)}) custom-call(bf16[128,2304]{1,0:T(8,128)(2,1)} %get-tuple-element.4.rows, f32[1,32,64]{2,1,0:T(8,128)} %get-tuple-element.5.cells), custom_call_target="tpu_custom_call" | custom-call | tf_op jit(solution)/shard_map/deliver/pallas_call | solution.py:596
